TPU v7x, 128 devices: a whole 4x4x4 slice. The times are simulated.
128 devices in a mesh: curve: 32 (over x, y, core), slab: 4 (over z).
Axes of the slice: x: 4, y: 4, z: 4, core: 2. Of those that a mesh axis runs over, the one named last changes fastest.
Arguments:
- start_state: float32 [135, 16384], P(None, ('curve', 'slab')), may hold values from -6 to 6
- right_side: float32 [135, 16384], P(None, ('curve', 'slab')), may hold values from -6 to 6
- block_inverse: float32 [135, 135, 16384], P(None, None, ('curve', 'slab')), as said below
- lifted_flux_jacobian: float32 [6, 135, 45], replicated, may hold values from -0.875 to 0.875
- face_weight: float32 [6, 16384], P(None, ('curve', 'slab')), may hold values from 0.1 to 0.4
- dep_level: int32 [16384], P(('curve', 'slab')), may hold values from 0 to 7
- face_link: int32 [6, 16384], P(None, ('curve', 'slab')), may hold values from -1 to 127, as said below
- send_list: int32 [8, 65536], P(None, ('curve', 'slab')), may hold values from 0 to 768, as said below
- recv_list: int32 [8, 65536], P(None, ('curve', 'slab')), may hold values from 0 to 768, as said below
Outputs:
- forward_state: float32 [135, 16384], P(None, ('curve', 'slab'))
- swept_state: float32 [135, 16384], P(None, ('curve', 'slab'))
Inputs may be any that keep to these rules, and one draw needn't show every extreme that they name: `block_inverse`: A dense 135 x 135 matrix for each element. `face_link`: for face d of element k of a device, the index on the same device of the element across that face, or -1 where that element lies on another device or outside the domain; links are mutual. `send_list`: A device's shard holds, for each level, 4 slots for each destination device in order; an entry d * 128 + k names face d of the device's local element k, and 768 marks an empty slot. Non-empty slots go only to devices whose curve index differs from the sender's by at most one. In every draw some device fills all 4 slots to one destination at every level. `recv_list`: A device's shard holds, for each level, 4 slots for each source device in order; slot j from source t names the face index at which t's slot j toward this device arrives, empty (768) exactly where that send slot is empty. Over all levels no face appears twice in one device's shard. Non-empty slots come only from devices whose curve index differs by at most one.
All inputs are finite; a program needn't handle non-finite values.
Results may differ from a plain program's by a relative error of at most 0.0003.
Values sent between devices are 32-bit elements; how exact they have to be, the bound alone decides.
A program may use at most 64 MiB of HBM per device.

v0:
```python
import jax
import jax.numpy as jnp
from jax import lax
from jax.sharding import PartitionSpec as P

VARS = 5
TRACE = 45


REVERSE_FACE = (1, 0, 3, 2, 5, 4)


def passed_along(block, axis, distance):
    devices = range(lax.axis_size(axis))
    route = [(i - distance, i) for i in devices if i - distance in devices]
    return lax.ppermute(block, axis, route)


def face_table(values):
    columns = values.shape[-1]
    cube = values.reshape(VARS, 3, 3, 3, columns)
    faces = [
        cube[:, 0],
        cube[:, 2],
        cube[:, :, 0],
        cube[:, :, 2],
        cube[:, :, :, 0],
        cube[:, :, :, 2],
    ]
    joined = jnp.concatenate([piece.reshape(TRACE, columns) for piece in faces], axis=1)
    return jnp.concatenate([joined, jnp.zeros((TRACE, 1), joined.dtype)], axis=1)


def neighbor_index(links):
    columns = links.shape[1]
    offsets = jnp.array(REVERSE_FACE, jnp.int32)[:, None] * columns
    return jnp.where(links >= 0, links + offsets, 6 * columns).reshape(6 * columns)


def inflow(traces, ghosts, where_from, lifted_flux_jacobian, coupling_weights):
    columns = coupling_weights.shape[1]
    gathered = (traces[:, where_from] + ghosts[:, : 6 * columns]).reshape(TRACE, 6, columns)
    weighted_traces = gathered * coupling_weights[None]
    return jnp.einsum(
        "vuh,hvw->uw", lifted_flux_jacobian, weighted_traces, precision=lax.Precision.HIGHEST
    )


def route_traces(packed, width):
    curve_count = lax.axis_size("curve")
    slab_count = lax.axis_size("slab")
    trace_rows = packed.shape[0]
    blocks = packed.reshape(trace_rows, curve_count, slab_count, width)
    padded = jnp.pad(blocks, ((0, 0), (1, 1), (0, 0), (0, 0)))
    own_curve = lax.axis_index("curve")
    nearby = lax.dynamic_slice_in_dim(padded, own_curve, 3, axis=1)
    swapped = lax.all_to_all(nearby, "slab", split_axis=2, concat_axis=2, tiled=True)
    from_below = passed_along(swapped[:, 2], "curve", 1)
    from_above = passed_along(swapped[:, 0], "curve", -1)
    arrived = jnp.stack([from_below, swapped[:, 1], from_above], axis=1)
    holder = lax.dynamic_update_slice_in_dim(jnp.zeros_like(padded), arrived, own_curve, axis=1)
    return holder[:, 1 : curve_count + 1].reshape(trace_rows, curve_count * slab_count * width)


def deliver_traces(ghosts, traces, sends, recvs, width):
    arrived = route_traces(traces[:, sends], width)
    return ghosts.at[:, recvs].set(arrived)


def body(
    start_state,
    right_side,
    block_inverse,
    lifted_flux_jacobian,
    face_weight,
    dep_level,
    face_link,
    send_list,
    recv_list,
):
    columns = start_state.shape[1]
    devices = lax.axis_size("curve") * lax.axis_size("slab")
    count_of_levels = send_list.shape[0]
    slot_count = send_list.shape[1] // devices
    where_from = neighbor_index(face_link)
    all_send = (
        send_list.reshape(count_of_levels, devices, slot_count)
        .transpose(1, 0, 2)
        .reshape(devices * count_of_levels * slot_count)
    )
    all_recv = (
        recv_list.reshape(count_of_levels, devices, slot_count)
        .transpose(1, 0, 2)
        .reshape(devices * count_of_levels * slot_count)
    )
    ghosts = jnp.zeros((TRACE, 6 * columns + 1), jnp.float32)
    traces = face_table(start_state)
    ghosts = deliver_traces(ghosts, traces, all_send, all_recv, count_of_levels * slot_count)

    def advance(current, ghosts, traces, level_now):
        flows = inflow(traces, ghosts, where_from, lifted_flux_jacobian, face_weight)
        update = jnp.einsum(
            "ije,je->ie", block_inverse, right_side - flows, precision=lax.Precision.HIGHEST
        )
        return jnp.where(dep_level[None] == level_now, update, current)

    def level_step(level_now, carried_state):
        current, ghosts, traces = carried_state
        current = advance(current, ghosts, traces, level_now)
        traces = face_table(current)
        sends = lax.dynamic_index_in_dim(send_list, level_now, 0, keepdims=False)
        recvs = lax.dynamic_index_in_dim(recv_list, level_now, 0, keepdims=False)
        ghosts = deliver_traces(ghosts, traces, sends, recvs, slot_count)
        return (current, ghosts, traces)

    def forward_step(step_now, carried_state):
        return level_step(step_now, carried_state)

    def backward_step(step_now, carried_state):
        return level_step(count_of_levels - 1 - step_now, carried_state)

    carried_state = lax.fori_loop(0, count_of_levels, forward_step, (start_state, ghosts, traces))
    forward_state = carried_state[0]
    current, ghosts, traces = lax.fori_loop(0, count_of_levels - 1, backward_step, carried_state)
    swept_state = advance(current, ghosts, traces, 0)
    return (forward_state, swept_state)


def solution(mesh):
    return jax.shard_map(
        body,
        mesh=mesh,
        in_specs=(
            P(None, ("curve", "slab")),
            P(None, ("curve", "slab")),
            P(None, None, ("curve", "slab")),
            P(),
            P(None, ("curve", "slab")),
            P(("curve", "slab")),
            P(None, ("curve", "slab")),
            P(None, ("curve", "slab")),
            P(None, ("curve", "slab")),
        ),
        out_specs=(P(None, ("curve", "slab")), P(None, ("curve", "slab"))),
        check_vma=False,
    )
```

profile of v0, /device:TPU:7, one launch (start us, length us, event | category | flops | bytes accessed | tf_op | source)
XLA Modules:
  0.0 512.1 jit_solution(9039737888249306071)
XLA Ops:
  4.2 10.8 %gather_fusion.4 = f32[4096,45]{1,0:T(8,128)S(1)} fusion(f32[45,769]{0,1:T(8,128)S(1)} %copy.104, s32[4096]{0:T(1024)S(1)} %broadcast_clamp_fusion), kind=kCustom, calls=%fused_computation.4 | custom fusion | bytes 1490944 | tf_op jit(solution)/shard_map/gather | solution.py:66
  17.3 5.0 all-to-all-start.2
  22.4 4.5 all-to-all-done.2
  28.4 5.2 %collective-permute-start.4 = (f32[45,4,32]{0,2,1:T(8,128)S(1)}, f32[45,4,32]{0,2,1:T(8,128)S(1)}, u32[]{:S(2)}, u32[]{:S(2)}) collective-permute-start(f32[45,4,32]{0,2,1:T(8,128)S(1)} %get-tuple-element.657), channel_id=1, source_target_pairs={{0,4},{4,8},{8,12},{12,16},{16,20},{20,24},{24,28},{28,32},{32,36}... | collective-permute-start | bytes 69128 | tf_op jit(solution)/shard_map/ppermute | solution.py:16
  33.6 1.9 collective-permute-start.5
  35.6 3.6 collective-permute-done.5
  39.8 10.9 %scatter_custom_fusion.2 = f32[45,769]{0,1:T(8,128)S(1)} fusion(s32[4096]{0:T(1024)S(1)} %bitcast.288, f32[4096,45]{1,0:T(8,128)S(1)} %bitcast.272, f32[]{:T(128)} %constant.211.clone.1), kind=kCustom, calls=%fused_computation.81 | custom fusion | bytes 138424 | tf_op jit(solution)/shard_map/scatter | solution.py:67
  50.7 241.0 %while.38 = (s32[]{:T(128)}, f32[135,128]{1,0:T(8,128)S(1)}, f32[45,769]{0,1:T(8,128)S(1)}, f32[45,769]{1,0:T(8,128)S(1)}, s32[128]{0:T(128)S(1)}, /*index=5*/s3...) while((s32[]{:T(128)}, f32[135,128]{1,0:T(8,128)S(1)}, ...), condition=%wide.region_3.4_spmd, body=%wide.region_1.3_spmd.sunk | while | flops 60751072 | bytes 13671031 | solution.py:122
  53.5 4.9 multiply_reduce_fusion.5
  61.0 6.5 %all_to_all.31 = f32[4,1,540]{2,1,0:T(1,128)S(1)} all-to-all(f32[4,1,540]{2,1,0:T(1,128)S(1)} %reshape.547), channel_id=1, replica_groups=mesh['curve'=32,'slab'=4] {'slab'}, dimensions={0} | all-to-all | bytes 17280 | tf_op jit(solution)/shard_map/while/body/eval_jaxpr/all_to_all | solution.py:57
  68.8 3.9 collective-permute-start
  72.8 1.9 collective-permute-start.1
  74.7 3.4 collective-permute-done.1
  82.8 4.9 multiply_reduce_fusion.5
  90.3 6.5 %all_to_all.31 = f32[4,1,540]{2,1,0:T(1,128)S(1)} all-to-all(f32[4,1,540]{2,1,0:T(1,128)S(1)} %reshape.547), channel_id=1, replica_groups=mesh['curve'=32,'slab'=4] {'slab'}, dimensions={0} | all-to-all | bytes 17280 | tf_op jit(solution)/shard_map/while/body/eval_jaxpr/all_to_all | solution.py:57
  98.1 7.6 %collective-permute-start = (f32[45,4,4]{0,2,1:T(4,128)S(1)}, f32[45,4,4]{0,2,1:T(4,128)S(1)}, u32[]{:S(2)}, u32[]{:S(2)}) collective-permute-start(f32[45,4,4]{0,2,1:T(4,128)S(1)} %get-tuple-element.830), channel_id=1, source_target_pairs={{4,0},{8,4},{12,8},{16,12},{20,16},{24,20},{28,24},{32,28},{36,32}... | collective-permute-start | bytes 8648 | tf_op jit(solution)/shard_map/while/body/eval_jaxpr/ppermute | solution.py:16
  113.5 4.9 multiply_reduce_fusion.5
  121.0 6.5 %all_to_all.31 = f32[4,1,540]{2,1,0:T(1,128)S(1)} all-to-all(f32[4,1,540]{2,1,0:T(1,128)S(1)} %reshape.547), channel_id=1, replica_groups=mesh['curve'=32,'slab'=4] {'slab'}, dimensions={0} | all-to-all | bytes 17280 | tf_op jit(solution)/shard_map/while/body/eval_jaxpr/all_to_all | solution.py:57
  128.8 7.1 %collective-permute-start = (f32[45,4,4]{0,2,1:T(4,128)S(1)}, f32[45,4,4]{0,2,1:T(4,128)S(1)}, u32[]{:S(2)}, u32[]{:S(2)}) collective-permute-start(f32[45,4,4]{0,2,1:T(4,128)S(1)} %get-tuple-element.830), channel_id=1, source_target_pairs={{4,0},{8,4},{12,8},{16,12},{20,16},{24,20},{28,24},{32,28},{36,32}... | collective-permute-start | bytes 8648 | tf_op jit(solution)/shard_map/while/body/eval_jaxpr/ppermute | solution.py:16
  135.9 1.9 collective-permute-start.1
  143.7 4.9 multiply_reduce_fusion.5
  151.2 6.5 %all_to_all.31 = f32[4,1,540]{2,1,0:T(1,128)S(1)} all-to-all(f32[4,1,540]{2,1,0:T(1,128)S(1)} %reshape.547), channel_id=1, replica_groups=mesh['curve'=32,'slab'=4] {'slab'}, dimensions={0} | all-to-all | bytes 17280 | tf_op jit(solution)/shard_map/while/body/eval_jaxpr/all_to_all | solution.py:57
  159.0 7.1 %collective-permute-start = (f32[45,4,4]{0,2,1:T(4,128)S(1)}, f32[45,4,4]{0,2,1:T(4,128)S(1)}, u32[]{:S(2)}, u32[]{:S(2)}) collective-permute-start(f32[45,4,4]{0,2,1:T(4,128)S(1)} %get-tuple-element.830), channel_id=1, source_target_pairs={{4,0},{8,4},{12,8},{16,12},{20,16},{24,20},{28,24},{32,28},{36,32}... | collective-permute-start | bytes 8648 | tf_op jit(solution)/shard_map/while/body/eval_jaxpr/ppermute | solution.py:16
  166.1 1.9 collective-permute-start.1
  173.9 4.9 multiply_reduce_fusion.5
  181.3 6.5 %all_to_all.31 = f32[4,1,540]{2,1,0:T(1,128)S(1)} all-to-all(f32[4,1,540]{2,1,0:T(1,128)S(1)} %reshape.547), channel_id=1, replica_groups=mesh['curve'=32,'slab'=4] {'slab'}, dimensions={0} | all-to-all | bytes 17280 | tf_op jit(solution)/shard_map/while/body/eval_jaxpr/all_to_all | solution.py:57
  189.2 7.1 %collective-permute-start = (f32[45,4,4]{0,2,1:T(4,128)S(1)}, f32[45,4,4]{0,2,1:T(4,128)S(1)}, u32[]{:S(2)}, u32[]{:S(2)}) collective-permute-start(f32[45,4,4]{0,2,1:T(4,128)S(1)} %get-tuple-element.830), channel_id=1, source_target_pairs={{4,0},{8,4},{12,8},{16,12},{20,16},{24,20},{28,24},{32,28},{36,32}... | collective-permute-start | bytes 8648 | tf_op jit(solution)/shard_map/while/body/eval_jaxpr/ppermute | solution.py:16
  204.1 4.9 multiply_reduce_fusion.5
  211.5 6.5 %all_to_all.31 = f32[4,1,540]{2,1,0:T(1,128)S(1)} all-to-all(f32[4,1,540]{2,1,0:T(1,128)S(1)} %reshape.547), channel_id=1, replica_groups=mesh['curve'=32,'slab'=4] {'slab'}, dimensions={0} | all-to-all | bytes 17280 | tf_op jit(solution)/shard_map/while/body/eval_jaxpr/all_to_all | solution.py:57
  219.3 7.1 %collective-permute-start = (f32[45,4,4]{0,2,1:T(4,128)S(1)}, f32[45,4,4]{0,2,1:T(4,128)S(1)}, u32[]{:S(2)}, u32[]{:S(2)}) collective-permute-start(f32[45,4,4]{0,2,1:T(4,128)S(1)} %get-tuple-element.830), channel_id=1, source_target_pairs={{4,0},{8,4},{12,8},{16,12},{20,16},{24,20},{28,24},{32,28},{36,32}... | collective-permute-start | bytes 8648 | tf_op jit(solution)/shard_map/while/body/eval_jaxpr/ppermute | solution.py:16
  234.2 4.9 multiply_reduce_fusion.5
  241.7 6.5 %all_to_all.31 = f32[4,1,540]{2,1,0:T(1,128)S(1)} all-to-all(f32[4,1,540]{2,1,0:T(1,128)S(1)} %reshape.547), channel_id=1, replica_groups=mesh['curve'=32,'slab'=4] {'slab'}, dimensions={0} | all-to-all | bytes 17280 | tf_op jit(solution)/shard_map/while/body/eval_jaxpr/all_to_all | solution.py:57
  249.5 7.1 %collective-permute-start = (f32[45,4,4]{0,2,1:T(4,128)S(1)}, f32[45,4,4]{0,2,1:T(4,128)S(1)}, u32[]{:S(2)}, u32[]{:S(2)}) collective-permute-start(f32[45,4,4]{0,2,1:T(4,128)S(1)} %get-tuple-element.830), channel_id=1, source_target_pairs={{4,0},{8,4},{12,8},{16,12},{20,16},{24,20},{28,24},{32,28},{36,32}... | collective-permute-start | bytes 8648 | tf_op jit(solution)/shard_map/while/body/eval_jaxpr/ppermute | solution.py:16
  256.6 1.9 collective-permute-start.1
  264.4 4.9 multiply_reduce_fusion.5
  271.9 6.5 %all_to_all.31 = f32[4,1,540]{2,1,0:T(1,128)S(1)} all-to-all(f32[4,1,540]{2,1,0:T(1,128)S(1)} %reshape.547), channel_id=1, replica_groups=mesh['curve'=32,'slab'=4] {'slab'}, dimensions={0} | all-to-all | bytes 17280 | tf_op jit(solution)/shard_map/while/body/eval_jaxpr/all_to_all | solution.py:57
  279.7 7.1 %collective-permute-start = (f32[45,4,4]{0,2,1:T(4,128)S(1)}, f32[45,4,4]{0,2,1:T(4,128)S(1)}, u32[]{:S(2)}, u32[]{:S(2)}) collective-permute-start(f32[45,4,4]{0,2,1:T(4,128)S(1)} %get-tuple-element.830), channel_id=1, source_target_pairs={{4,0},{8,4},{12,8},{16,12},{20,16},{24,20},{28,24},{32,28},{36,32}... | collective-permute-start | bytes 8648 | tf_op jit(solution)/shard_map/while/body/eval_jaxpr/ppermute | solution.py:16
  292.4 211.4 %while.39 = (s32[]{:T(128)}, f32[135,128]{1,0:T(8,128)S(1)}, f32[45,769]{0,1:T(8,128)S(1)}, f32[45,769]{1,0:T(8,128)S(1)}, s32[128]{0:T(128)S(1)}, /*index=5*/s3...) while((s32[]{:T(128)}, f32[135,128]{1,0:T(8,128)S(1)}, ...), condition=%wide.region_6.7_spmd, body=%wide.region_4.6_spmd.sunk | while | flops 60751072 | bytes 13671093 | solution.py:124
  295.2 4.9 multiply_reduce_fusion.6
  302.7 6.5 %all_to_all.32 = f32[4,1,540]{2,1,0:T(1,128)S(1)} all-to-all(f32[4,1,540]{2,1,0:T(1,128)S(1)} %reshape.557), channel_id=1, replica_groups=mesh['curve'=32,'slab'=4] {'slab'}, dimensions={0} | all-to-all | bytes 17280 | tf_op jit(solution)/shard_map/while/body/eval_jaxpr/all_to_all | solution.py:57
  310.5 7.1 %collective-permute-start.2 = (f32[45,4,4]{0,2,1:T(4,128)S(1)}, f32[45,4,4]{0,2,1:T(4,128)S(1)}, u32[]{:S(2)}, u32[]{:S(2)}) collective-permute-start(f32[45,4,4]{0,2,1:T(4,128)S(1)} %get-tuple-element.853), channel_id=1, source_target_pairs={{4,0},{8,4},{12,8},{16,12},{20,16},{24,20},{28,24},{32,28},{36,32}... | collective-permute-start | bytes 8648 | tf_op jit(solution)/shard_map/while/body/eval_jaxpr/ppermute | solution.py:16
  317.6 1.9 collective-permute-start.3
  325.4 4.9 multiply_reduce_fusion.6
  332.9 6.5 %all_to_all.32 = f32[4,1,540]{2,1,0:T(1,128)S(1)} all-to-all(f32[4,1,540]{2,1,0:T(1,128)S(1)} %reshape.557), channel_id=1, replica_groups=mesh['curve'=32,'slab'=4] {'slab'}, dimensions={0} | all-to-all | bytes 17280 | tf_op jit(solution)/shard_map/while/body/eval_jaxpr/all_to_all | solution.py:57
  340.7 7.1 %collective-permute-start.2 = (f32[45,4,4]{0,2,1:T(4,128)S(1)}, f32[45,4,4]{0,2,1:T(4,128)S(1)}, u32[]{:S(2)}, u32[]{:S(2)}) collective-permute-start(f32[45,4,4]{0,2,1:T(4,128)S(1)} %get-tuple-element.853), channel_id=1, source_target_pairs={{4,0},{8,4},{12,8},{16,12},{20,16},{24,20},{28,24},{32,28},{36,32}... | collective-permute-start | bytes 8648 | tf_op jit(solution)/shard_map/while/body/eval_jaxpr/ppermute | solution.py:16
  347.8 1.9 collective-permute-start.3
  355.6 4.9 multiply_reduce_fusion.6
  363.1 6.5 %all_to_all.32 = f32[4,1,540]{2,1,0:T(1,128)S(1)} all-to-all(f32[4,1,540]{2,1,0:T(1,128)S(1)} %reshape.557), channel_id=1, replica_groups=mesh['curve'=32,'slab'=4] {'slab'}, dimensions={0} | all-to-all | bytes 17280 | tf_op jit(solution)/shard_map/while/body/eval_jaxpr/all_to_all | solution.py:57
  370.9 7.1 %collective-permute-start.2 = (f32[45,4,4]{0,2,1:T(4,128)S(1)}, f32[45,4,4]{0,2,1:T(4,128)S(1)}, u32[]{:S(2)}, u32[]{:S(2)}) collective-permute-start(f32[45,4,4]{0,2,1:T(4,128)S(1)} %get-tuple-element.853), channel_id=1, source_target_pairs={{4,0},{8,4},{12,8},{16,12},{20,16},{24,20},{28,24},{32,28},{36,32}... | collective-permute-start | bytes 8648 | tf_op jit(solution)/shard_map/while/body/eval_jaxpr/ppermute | solution.py:16
  378.0 1.9 collective-permute-start.3
  385.8 4.9 multiply_reduce_fusion.6
  393.3 6.5 %all_to_all.32 = f32[4,1,540]{2,1,0:T(1,128)S(1)} all-to-all(f32[4,1,540]{2,1,0:T(1,128)S(1)} %reshape.557), channel_id=1, replica_groups=mesh['curve'=32,'slab'=4] {'slab'}, dimensions={0} | all-to-all | bytes 17280 | tf_op jit(solution)/shard_map/while/body/eval_jaxpr/all_to_all | solution.py:57
  401.1 7.1 %collective-permute-start.2 = (f32[45,4,4]{0,2,1:T(4,128)S(1)}, f32[45,4,4]{0,2,1:T(4,128)S(1)}, u32[]{:S(2)}, u32[]{:S(2)}) collective-permute-start(f32[45,4,4]{0,2,1:T(4,128)S(1)} %get-tuple-element.853), channel_id=1, source_target_pairs={{4,0},{8,4},{12,8},{16,12},{20,16},{24,20},{28,24},{32,28},{36,32}... | collective-permute-start | bytes 8648 | tf_op jit(solution)/shard_map/while/body/eval_jaxpr/ppermute | solution.py:16
  416.0 4.9 multiply_reduce_fusion.6
  423.5 6.5 %all_to_all.32 = f32[4,1,540]{2,1,0:T(1,128)S(1)} all-to-all(f32[4,1,540]{2,1,0:T(1,128)S(1)} %reshape.557), channel_id=1, replica_groups=mesh['curve'=32,'slab'=4] {'slab'}, dimensions={0} | all-to-all | bytes 17280 | tf_op jit(solution)/shard_map/while/body/eval_jaxpr/all_to_all | solution.py:57
  431.3 7.1 %collective-permute-start.2 = (f32[45,4,4]{0,2,1:T(4,128)S(1)}, f32[45,4,4]{0,2,1:T(4,128)S(1)}, u32[]{:S(2)}, u32[]{:S(2)}) collective-permute-start(f32[45,4,4]{0,2,1:T(4,128)S(1)} %get-tuple-element.853), channel_id=1, source_target_pairs={{4,0},{8,4},{12,8},{16,12},{20,16},{24,20},{28,24},{32,28},{36,32}... | collective-permute-start | bytes 8648 | tf_op jit(solution)/shard_map/while/body/eval_jaxpr/ppermute | solution.py:16
  446.2 4.9 multiply_reduce_fusion.6
  453.7 6.5 %all_to_all.32 = f32[4,1,540]{2,1,0:T(1,128)S(1)} all-to-all(f32[4,1,540]{2,1,0:T(1,128)S(1)} %reshape.557), channel_id=1, replica_groups=mesh['curve'=32,'slab'=4] {'slab'}, dimensions={0} | all-to-all | bytes 17280 | tf_op jit(solution)/shard_map/while/body/eval_jaxpr/all_to_all | solution.py:57
  461.5 7.1 %collective-permute-start.2 = (f32[45,4,4]{0,2,1:T(4,128)S(1)}, f32[45,4,4]{0,2,1:T(4,128)S(1)}, u32[]{:S(2)}, u32[]{:S(2)}) collective-permute-start(f32[45,4,4]{0,2,1:T(4,128)S(1)} %get-tuple-element.853), channel_id=1, source_target_pairs={{4,0},{8,4},{12,8},{16,12},{20,16},{24,20},{28,24},{32,28},{36,32}... | collective-permute-start | bytes 8648 | tf_op jit(solution)/shard_map/while/body/eval_jaxpr/ppermute | solution.py:16
  468.6 1.9 collective-permute-start.3
  476.4 4.9 multiply_reduce_fusion.6
  483.9 6.5 %all_to_all.32 = f32[4,1,540]{2,1,0:T(1,128)S(1)} all-to-all(f32[4,1,540]{2,1,0:T(1,128)S(1)} %reshape.557), channel_id=1, replica_groups=mesh['curve'=32,'slab'=4] {'slab'}, dimensions={0} | all-to-all | bytes 17280 | tf_op jit(solution)/shard_map/while/body/eval_jaxpr/all_to_all | solution.py:57
  491.7 7.1 %collective-permute-start.2 = (f32[45,4,4]{0,2,1:T(4,128)S(1)}, f32[45,4,4]{0,2,1:T(4,128)S(1)}, u32[]{:S(2)}, u32[]{:S(2)}) collective-permute-start(f32[45,4,4]{0,2,1:T(4,128)S(1)} %get-tuple-element.853), channel_id=1, source_target_pairs={{4,0},{8,4},{12,8},{16,12},{20,16},{24,20},{28,24},{32,28},{36,32}... | collective-permute-start | bytes 8648 | tf_op jit(solution)/shard_map/while/body/eval_jaxpr/ppermute | solution.py:16
  506.6 4.9 multiply_reduce_fusion.2
  (701 shorter events, 166.6 us)
Async XLA Ops:
  15.0 0.9 copy-start.4
  15.0 2.3 copy-start.7
  15.0 2.3 copy-start.5
  15.0 2.3 copy-start.6
  17.3 9.5 %all-to-all-start.2 = ((f32[4,1,4320]{2,1,0:T(1,128)}), f32[4,1,4320]{2,1,0:T(1,128)S(1)}, u32[]{:S(2)}, u32[]{:S(2)}) async-start(f32[4,1,4320]{2,1,0:T(1,128)} %reshape.517), calls=%async_computation.2 | async-start | bytes 139264 | tf_op jit(solution)/shard_map/all_to_all | solution.py:57
  28.4 7.1 %collective-permute-start.4 = (f32[45,4,32]{0,2,1:T(8,128)S(1)}, f32[45,4,32]{0,2,1:T(8,128)S(1)}, u32[]{:S(2)}, u32[]{:S(2)}) collective-permute-start(f32[45,4,32]{0,2,1:T(8,128)S(1)} %get-tuple-element.657), channel_id=1, source_target_pairs={{0,4},{4,8},{8,12},{12,16},{16,20},{20,24},{24,28},{28,32},{32,36}... | collective-permute-start | bytes 69128 | tf_op jit(solution)/shard_map/ppermute | solution.py:16
  33.6 5.6 %collective-permute-start.5 = (f32[45,4,32]{0,2,1:T(8,128)S(1)}, f32[45,4,32]{0,2,1:T(8,128)S(1)}, u32[]{:S(2)}, u32[]{:S(2)}) collective-permute-start(f32[45,4,32]{0,2,1:T(8,128)S(1)} %get-tuple-element.658), channel_id=1, source_target_pairs={{4,0},{8,4},{12,8},{16,12},{20,16},{24,20},{28,24},{32,28},{36,32}... | collective-permute-start | bytes 69128 | tf_op jit(solution)/shard_map/ppermute | solution.py:16
  39.5 11.2 %copy-start = (f32[6,135,45]{1,2,0:T(8,128)S(1)}, f32[6,135,45]{1,2,0:T(8,128)}, u32[]{:S(2)}) copy-start(f32[6,135,45]{1,2,0:T(8,128)} %param.17) | copy-start | bytes 437404
  39.5 11.2 %copy-start.2 = (f32[135,128]{1,0:T(8,128)S(1)}, f32[135,128]{1,0:T(8,128)}, u32[]{:S(2)}) copy-start(f32[135,128]{1,0:T(8,128)} %param.15) | copy-start | bytes 207364
  39.6 11.2 %copy-start.3 = (f32[6,128]{1,0:T(8,128)S(1)}, f32[6,128]{1,0:T(8,128)}, u32[]{:S(2)}) copy-start(f32[6,128]{1,0:T(8,128)} %param.18) | copy-start | bytes 9220
  68.8 5.9 %collective-permute-start = (f32[45,4,4]{0,2,1:T(4,128)S(1)}, f32[45,4,4]{0,2,1:T(4,128)S(1)}, u32[]{:S(2)}, u32[]{:S(2)}) collective-permute-start(f32[45,4,4]{0,2,1:T(4,128)S(1)} %get-tuple-element.830), channel_id=1, source_target_pairs={{4,0},{8,4},{12,8},{16,12},{20,16},{24,20},{28,24},{32,28},{36,32}... | collective-permute-start | bytes 8648 | tf_op jit(solution)/shard_map/while/body/eval_jaxpr/ppermute | solution.py:16
  72.8 5.3 %collective-permute-start.1 = (f32[45,4,4]{0,2,1:T(4,128)S(1)}, f32[45,4,4]{0,2,1:T(4,128)S(1)}, u32[]{:S(2)}, u32[]{:S(2)}) collective-permute-start(f32[45,4,4]{0,2,1:T(4,128)S(1)} %get-tuple-element.832), channel_id=1, source_target_pairs={{0,4},{4,8},{8,12},{12,16},{16,20},{20,24},{24,28},{28,32},{32,36}... | collective-permute-start | bytes 8648 | tf_op jit(solution)/shard_map/while/body/eval_jaxpr/ppermute | solution.py:16
  98.1 9.5 %collective-permute-start = (f32[45,4,4]{0,2,1:T(4,128)S(1)}, f32[45,4,4]{0,2,1:T(4,128)S(1)}, u32[]{:S(2)}, u32[]{:S(2)}) collective-permute-start(f32[45,4,4]{0,2,1:T(4,128)S(1)} %get-tuple-element.830), channel_id=1, source_target_pairs={{4,0},{8,4},{12,8},{16,12},{20,16},{24,20},{28,24},{32,28},{36,32}... | collective-permute-start | bytes 8648 | tf_op jit(solution)/shard_map/while/body/eval_jaxpr/ppermute | solution.py:16
  105.7 3.1 collective-permute-start.1
  128.8 9.0 %collective-permute-start = (f32[45,4,4]{0,2,1:T(4,128)S(1)}, f32[45,4,4]{0,2,1:T(4,128)S(1)}, u32[]{:S(2)}, u32[]{:S(2)}) collective-permute-start(f32[45,4,4]{0,2,1:T(4,128)S(1)} %get-tuple-element.830), channel_id=1, source_target_pairs={{4,0},{8,4},{12,8},{16,12},{20,16},{24,20},{28,24},{32,28},{36,32}... | collective-permute-start | bytes 8648 | tf_op jit(solution)/shard_map/while/body/eval_jaxpr/ppermute | solution.py:16
  135.9 3.1 collective-permute-start.1
  159.0 9.0 %collective-permute-start = (f32[45,4,4]{0,2,1:T(4,128)S(1)}, f32[45,4,4]{0,2,1:T(4,128)S(1)}, u32[]{:S(2)}, u32[]{:S(2)}) collective-permute-start(f32[45,4,4]{0,2,1:T(4,128)S(1)} %get-tuple-element.830), channel_id=1, source_target_pairs={{4,0},{8,4},{12,8},{16,12},{20,16},{24,20},{28,24},{32,28},{36,32}... | collective-permute-start | bytes 8648 | tf_op jit(solution)/shard_map/while/body/eval_jaxpr/ppermute | solution.py:16
  166.1 3.1 collective-permute-start.1
  189.2 9.0 %collective-permute-start = (f32[45,4,4]{0,2,1:T(4,128)S(1)}, f32[45,4,4]{0,2,1:T(4,128)S(1)}, u32[]{:S(2)}, u32[]{:S(2)}) collective-permute-start(f32[45,4,4]{0,2,1:T(4,128)S(1)} %get-tuple-element.830), channel_id=1, source_target_pairs={{4,0},{8,4},{12,8},{16,12},{20,16},{24,20},{28,24},{32,28},{36,32}... | collective-permute-start | bytes 8648 | tf_op jit(solution)/shard_map/while/body/eval_jaxpr/ppermute | solution.py:16
  196.3 3.1 collective-permute-start.1
  219.3 9.0 %collective-permute-start = (f32[45,4,4]{0,2,1:T(4,128)S(1)}, f32[45,4,4]{0,2,1:T(4,128)S(1)}, u32[]{:S(2)}, u32[]{:S(2)}) collective-permute-start(f32[45,4,4]{0,2,1:T(4,128)S(1)} %get-tuple-element.830), channel_id=1, source_target_pairs={{4,0},{8,4},{12,8},{16,12},{20,16},{24,20},{28,24},{32,28},{36,32}... | collective-permute-start | bytes 8648 | tf_op jit(solution)/shard_map/while/body/eval_jaxpr/ppermute | solution.py:16
  226.4 3.1 collective-permute-start.1
  249.5 9.0 %collective-permute-start = (f32[45,4,4]{0,2,1:T(4,128)S(1)}, f32[45,4,4]{0,2,1:T(4,128)S(1)}, u32[]{:S(2)}, u32[]{:S(2)}) collective-permute-start(f32[45,4,4]{0,2,1:T(4,128)S(1)} %get-tuple-element.830), channel_id=1, source_target_pairs={{4,0},{8,4},{12,8},{16,12},{20,16},{24,20},{28,24},{32,28},{36,32}... | collective-permute-start | bytes 8648 | tf_op jit(solution)/shard_map/while/body/eval_jaxpr/ppermute | solution.py:16
  256.6 3.1 collective-permute-start.1
  279.7 9.0 %collective-permute-start = (f32[45,4,4]{0,2,1:T(4,128)S(1)}, f32[45,4,4]{0,2,1:T(4,128)S(1)}, u32[]{:S(2)}, u32[]{:S(2)}) collective-permute-start(f32[45,4,4]{0,2,1:T(4,128)S(1)} %get-tuple-element.830), channel_id=1, source_target_pairs={{4,0},{8,4},{12,8},{16,12},{20,16},{24,20},{28,24},{32,28},{36,32}... | collective-permute-start | bytes 8648 | tf_op jit(solution)/shard_map/while/body/eval_jaxpr/ppermute | solution.py:16
  286.8 3.1 collective-permute-start.1
  291.8 0.6 copy-start.1
  310.5 9.0 %collective-permute-start.2 = (f32[45,4,4]{0,2,1:T(4,128)S(1)}, f32[45,4,4]{0,2,1:T(4,128)S(1)}, u32[]{:S(2)}, u32[]{:S(2)}) collective-permute-start(f32[45,4,4]{0,2,1:T(4,128)S(1)} %get-tuple-element.853), channel_id=1, source_target_pairs={{4,0},{8,4},{12,8},{16,12},{20,16},{24,20},{28,24},{32,28},{36,32}... | collective-permute-start | bytes 8648 | tf_op jit(solution)/shard_map/while/body/eval_jaxpr/ppermute | solution.py:16
  317.6 3.1 collective-permute-start.3
  340.7 9.0 %collective-permute-start.2 = (f32[45,4,4]{0,2,1:T(4,128)S(1)}, f32[45,4,4]{0,2,1:T(4,128)S(1)}, u32[]{:S(2)}, u32[]{:S(2)}) collective-permute-start(f32[45,4,4]{0,2,1:T(4,128)S(1)} %get-tuple-element.853), channel_id=1, source_target_pairs={{4,0},{8,4},{12,8},{16,12},{20,16},{24,20},{28,24},{32,28},{36,32}... | collective-permute-start | bytes 8648 | tf_op jit(solution)/shard_map/while/body/eval_jaxpr/ppermute | solution.py:16
  347.8 3.1 collective-permute-start.3
  370.9 9.0 %collective-permute-start.2 = (f32[45,4,4]{0,2,1:T(4,128)S(1)}, f32[45,4,4]{0,2,1:T(4,128)S(1)}, u32[]{:S(2)}, u32[]{:S(2)}) collective-permute-start(f32[45,4,4]{0,2,1:T(4,128)S(1)} %get-tuple-element.853), channel_id=1, source_target_pairs={{4,0},{8,4},{12,8},{16,12},{20,16},{24,20},{28,24},{32,28},{36,32}... | collective-permute-start | bytes 8648 | tf_op jit(solution)/shard_map/while/body/eval_jaxpr/ppermute | solution.py:16
  378.0 3.1 collective-permute-start.3
  401.1 9.0 %collective-permute-start.2 = (f32[45,4,4]{0,2,1:T(4,128)S(1)}, f32[45,4,4]{0,2,1:T(4,128)S(1)}, u32[]{:S(2)}, u32[]{:S(2)}) collective-permute-start(f32[45,4,4]{0,2,1:T(4,128)S(1)} %get-tuple-element.853), channel_id=1, source_target_pairs={{4,0},{8,4},{12,8},{16,12},{20,16},{24,20},{28,24},{32,28},{36,32}... | collective-permute-start | bytes 8648 | tf_op jit(solution)/shard_map/while/body/eval_jaxpr/ppermute | solution.py:16
  408.2 3.1 collective-permute-start.3
  431.3 9.0 %collective-permute-start.2 = (f32[45,4,4]{0,2,1:T(4,128)S(1)}, f32[45,4,4]{0,2,1:T(4,128)S(1)}, u32[]{:S(2)}, u32[]{:S(2)}) collective-permute-start(f32[45,4,4]{0,2,1:T(4,128)S(1)} %get-tuple-element.853), channel_id=1, source_target_pairs={{4,0},{8,4},{12,8},{16,12},{20,16},{24,20},{28,24},{32,28},{36,32}... | collective-permute-start | bytes 8648 | tf_op jit(solution)/shard_map/while/body/eval_jaxpr/ppermute | solution.py:16
  438.4 3.1 collective-permute-start.3
  461.5 9.0 %collective-permute-start.2 = (f32[45,4,4]{0,2,1:T(4,128)S(1)}, f32[45,4,4]{0,2,1:T(4,128)S(1)}, u32[]{:S(2)}, u32[]{:S(2)}) collective-permute-start(f32[45,4,4]{0,2,1:T(4,128)S(1)} %get-tuple-element.853), channel_id=1, source_target_pairs={{4,0},{8,4},{12,8},{16,12},{20,16},{24,20},{28,24},{32,28},{36,32}... | collective-permute-start | bytes 8648 | tf_op jit(solution)/shard_map/while/body/eval_jaxpr/ppermute | solution.py:16
  468.6 3.1 collective-permute-start.3
  491.7 9.0 %collective-permute-start.2 = (f32[45,4,4]{0,2,1:T(4,128)S(1)}, f32[45,4,4]{0,2,1:T(4,128)S(1)}, u32[]{:S(2)}, u32[]{:S(2)}) collective-permute-start(f32[45,4,4]{0,2,1:T(4,128)S(1)} %get-tuple-element.853), channel_id=1, source_target_pairs={{4,0},{8,4},{12,8},{16,12},{20,16},{24,20},{28,24},{32,28},{36,32}... | collective-permute-start | bytes 8648 | tf_op jit(solution)/shard_map/while/body/eval_jaxpr/ppermute | solution.py:16
  498.8 3.1 collective-permute-start.3
where the time goes:
time: 519 us; the launch traced here: 512 us
  starting transfers between devices  145 us (28%)
  local copies, waits for them, and re-layouts  122 us (24%)
  other arithmetic  103 us (20%)
  blocking collectives  97.8 us (19%)
  waiting for transfers between devices  27.3 us (5%)
  matrix products  12.3 us (2%)
    ppermute x32, starting transfers between devices, passed_along(): return lax.ppermute(block, axis, route)  140 us
    all_to_all x15, blocking collectives, route_traces(): lax.all_to_all(nearby, 'slab', split_axis=2, concat_axis=2, tiled=True)  97.8 us
    dot_general x16, other arithmetic, advance(): jnp.einsum('ije,je->ie', block_inverse, right_side - flows, precision=lax...  78.1 us
    scatter x16, local copies, waits for them, and re-layouts, deliver_traces(): return ghosts.at[:, recvs].set(arrived)  38.2 us
    gather x16, local copies, waits for them, and re-layouts, deliver_traces(): arrived = route_traces(traces[:, sends], width)  26.3 us
    gather x16, local copies, waits for them, and re-layouts, inflow(): traces[:, where_from] + ghosts[:, :6 * columns]  25.2 us
    ppermute x32, waiting for transfers between devices, passed_along(): return lax.ppermute(block, axis, route)  22.8 us
    dot_general x16, matrix products, inflow(): jnp.einsum('vuh,hvw->uw', lifted_flux_jacobian, weighted_traces, precisio...  12.3 us
  transfers between devices with their start and end apart: 33, of which 17 were waited for; matrix products, arithmetic and copies ran while one was open for 0% of the time, Pallas kernels for 0%

commit v1 on v0

v1 whole, which is shorter than its diff:
```python
import functools

import jax
import jax.numpy as jnp
from jax import lax
from jax.experimental import pallas as pl
from jax.experimental.pallas import tpu as pltpu
from jax.sharding import PartitionSpec as P

VARS = 5
TRACE = 45
BLOCK = 135
EL = 128
LEVELS = 8
CAP = 4
PAD = 64
GROUPS = 12
ROWS = 8 * GROUPS
MESH = pl.DeviceIdType.MESH
F32 = jnp.float32
BF16 = jnp.bfloat16


def split(x):
    hi = x.astype(BF16)
    lo = (x - hi.astype(F32)).astype(BF16)
    return hi, lo


def dot(a, b):
    return lax.dot_general(a, b, (((1,), (0,)), ((), ())), preferred_element_type=F32)


def dot_t(a, b):
    return lax.dot_general(a, b, (((1,), (1,)), ((), ())), preferred_element_type=F32)


def kernel(
    start_ref,
    right_ref,
    inverse_hbm,
    jac_ref,
    weight_ref,
    level_ref,
    link_ref,
    send_ref,
    recv_ref,
    forward_ref,
    swept_ref,
    inverse,
    state,
    table,
    solve_in,
    base,
    update,
    jac,
    jac3,
    links,
    picks,
    drops,
    factors,
    flows,
    index,
    out_buf,
    in_buf,
    first_out,
    first_in,
    inverse_sem,
    send_sem,
    recv_sem,
    first_send_sem,
    first_recv_sem,
):
    curves = lax.axis_size("curve")
    slabs = lax.axis_size("slab")
    my_curve = lax.axis_index("curve")
    my_slab = lax.axis_index("slab")
    own_group = slabs + my_slab

    pull = pltpu.make_async_copy(inverse_hbm, inverse, inverse_sem)
    pull.start()
    in_buf[...] = jnp.zeros_like(in_buf)
    first_in[...] = jnp.zeros_like(first_in)

    def each_peer(act):
        @pl.when(my_curve > 0)
        def _():
            for z in range(slabs):
                act(-1, z)

        @pl.when(my_curve < curves - 1)
        def _():
            for z in range(slabs):
                act(1, z)

        for shift in range(1, slabs):
            act(0, lax.rem(my_slab + shift, slabs))

    barrier = pltpu.get_barrier_semaphore()
    each_peer(
        lambda step, z: pl.semaphore_signal(
            barrier, inc=1, device_id=(my_curve + step, z), device_id_type=MESH
        )
    )

    lane = lax.broadcasted_iota(jnp.int32, (ROWS, EL), 1)

    def to_rows(list_ref):
        shift = lax.rem((curves + 1 - my_curve) * (slabs * CAP), curves * slabs * CAP)
        near = pltpu.roll(list_ref[...], shift, 1)[:, :EL]
        tall = jnp.concatenate([near] * 16, axis=0).T
        index[...] = jnp.full_like(index, 6 * EL)
        for group in range(GROUPS):
            index[8 * group : 8 * group + CAP, :] = tall[CAP * group : CAP * (group + 1), :]

    table[...] = jnp.zeros_like(table)

    def fill_table():
        for side in range(2):
            for q in range(9):
                table[side, pl.ds(q, VARS, stride=9), :] = state[
                    pl.ds(18 * side + q, VARS, stride=27), :
                ]
            for q in range(3):
                table[2 + side, pl.ds(q, 15, stride=3), :] = state[
                    pl.ds(6 * side + q, 15, stride=9), :
                ]
            table[4 + side, :TRACE, :] = state[pl.ds(2 * side, TRACE, stride=3), :]

    state[...] = start_ref[...]
    fill_table()
    to_rows(send_ref)
    for level in range(LEVELS):
        column = index[:, level : level + 1]
        for face in range(6):
            picks[level, :, EL * face : EL * (face + 1)] = (
                jnp.where(column == lane + EL * face, 1.0, 0.0).astype(BF16)
            )

    def packed(level):
        hi, lo = split(jnp.concatenate([table[face] for face in range(6)], axis=1))
        both = jnp.concatenate([hi, lo], axis=1)
        twice = jnp.concatenate([both, both], axis=0)
        pick = picks[level]
        return dot_t(jnp.concatenate([pick, pick], axis=1), twice)

    for level in range(LEVELS):
        first_out[level] = packed(level).reshape(GROUPS, 8, EL)

    @pl.when(jnp.logical_and(my_curve > 0, my_curve < curves - 1))
    def _():
        pl.semaphore_wait(barrier, 3 * slabs - 1)

    @pl.when(jnp.logical_or(my_curve == 0, my_curve == curves - 1))
    def _():
        pl.semaphore_wait(barrier, 2 * slabs - 1)

    def first_copy(step, z):
        return pltpu.make_async_remote_copy(
            src_ref=first_out.at[:, (1 + step) * slabs + z],
            dst_ref=first_in.at[:, (1 - step) * slabs + my_slab],
            send_sem=first_send_sem.at[(1 + step) * slabs + z],
            recv_sem=first_recv_sem.at[(1 - step) * slabs + my_slab],
            device_id=(my_curve + step, z),
            device_id_type=MESH,
        )

    def first_arrival(step, z):
        group = (1 + step) * slabs + z
        return pltpu.make_async_remote_copy(
            src_ref=first_out.at[:, group],
            dst_ref=first_in.at[:, group],
            send_sem=first_send_sem.at[group],
            recv_sem=first_recv_sem.at[group],
            device_id=(my_curve + step, z),
            device_id_type=MESH,
        )

    def copy(slot, step, z):
        return pltpu.make_async_remote_copy(
            src_ref=out_buf.at[slot, (1 + step) * slabs + z],
            dst_ref=in_buf.at[slot, (1 - step) * slabs + my_slab],
            send_sem=send_sem.at[slot, (1 + step) * slabs + z],
            recv_sem=recv_sem.at[slot, (1 - step) * slabs + my_slab],
            device_id=(my_curve + step, z),
            device_id_type=MESH,
        )

    def arrival(slot, step, z):
        group = (1 + step) * slabs + z
        return pltpu.make_async_remote_copy(
            src_ref=out_buf.at[slot, group],
            dst_ref=in_buf.at[slot, group],
            send_sem=send_sem.at[slot, group],
            recv_sem=recv_sem.at[slot, group],
            device_id=(my_curve + step, z),
            device_id_type=MESH,
        )

    each_peer(lambda step, z: first_copy(step, z).start())
    first_in[:, own_group] = first_out[:, own_group]

    jac[...] = jnp.zeros_like(jac)
    for face in range(6):
        jac[:, PAD * face : PAD * face + TRACE] = jac_ref[face]
    jac_hi, jac_lo = split(jac[...])
    width = 6 * PAD
    jac3[:, :width] = jac_hi
    jac3[:, width : 2 * width] = jac_lo
    jac3[:, 2 * width :] = jac_hi

    row = lax.broadcasted_iota(jnp.int32, (EL, EL), 0)
    for face in range(6):
        one = jnp.where(link_ref[face : face + 1, :] == row, 1.0, 0.0).astype(BF16)
        links[face, :EL, :] = one
        links[face, EL:, :] = one

    to_rows(recv_ref)
    face_lane = lax.broadcasted_iota(jnp.int32, (ROWS, width), 1) // PAD
    for level in range(LEVELS):
        column = index[:, level : level + 1]
        hit = jnp.zeros((ROWS, EL), F32)
        gain = jnp.zeros((ROWS, EL), F32)
        for face in range(6):
            mine = column == lane + EL * face
            hit = jnp.where(mine, 1.0, hit)
            gain = jnp.where(mine, weight_ref[face : face + 1, :], gain)
        one = hit.astype(BF16)
        drops[level, :ROWS, :] = one
        drops[level, ROWS:, :] = one
        scale = jnp.sum(gain, axis=1, keepdims=True)
        factors[level] = jnp.where(column // EL == face_lane, scale, 0.0)

    def local_flow():
        parts_hi = []
        parts_lo = []
        for face in range(6):
            other = face + 1 - 2 * (face % 2)
            hi, lo = split(table[other])
            moved = dot(jnp.concatenate([hi, lo], axis=1), links[face])
            hi, lo = split(moved * weight_ref[face : face + 1, :])
            parts_hi.append(hi)
            parts_lo.append(lo)
        hi = jnp.concatenate(parts_hi, axis=0)
        lo = jnp.concatenate(parts_lo, axis=0)
        return dot(jac3[...], jnp.concatenate([hi, hi, lo], axis=0))

    def ghost_flow(level, block):
        thrice = jnp.concatenate([block] * 3, axis=1) * factors[level]
        hi, lo = split(thrice)
        spread = dot_t(jac3[...], jnp.concatenate([hi, hi, lo], axis=1))
        hi, lo = split(spread)
        return dot(jnp.concatenate([hi, lo], axis=1), drops[level])

    local = local_flow()
    each_peer(lambda step, z: first_arrival(step, z).wait_recv())
    known = right_ref[...] - local
    for level in range(LEVELS):
        flow = ghost_flow(level, first_in[level].reshape(ROWS, EL))
        flows[level] = flow
        known = known - flow
    solve_in[...] = known
    pull.wait()

    chunk = 9

    def advance(level):
        vector = solve_in[...]

        def rows(at, carry):
            for k in range(chunk):
                i = at * chunk + k
                update[pl.ds(i, 1), :] = jnp.sum(inverse[i] * vector, axis=0, keepdims=True)
            return carry

        lax.fori_loop(0, BLOCK // chunk, rows, 0)
        state[...] = jnp.where(level_ref[...] == level, update[...], state[...])

    def level_step(step, carry):
        level = jnp.where(step < LEVELS, step, 2 * LEVELS - 1 - step)
        slot = lax.rem(step, 2)
        advance(level)

        @pl.when(step >= 2)
        def _():
            each_peer(lambda s, z: arrival(slot, s, z).wait_send())

        fill_table()
        out_buf[slot] = packed(level).reshape(GROUPS, 8, EL)
        each_peer(lambda s, z: copy(slot, s, z).start())
        in_buf[slot, own_group] = out_buf[slot, own_group]

        @pl.when(step == LEVELS - 1)
        def _():
            forward_ref[...] = state[...]

        known = right_ref[...] - local_flow()
        for other in range(LEVELS):
            known = known - jnp.where(level == other, 0.0, flows[other])
        base[...] = known
        each_peer(lambda s, z: arrival(slot, s, z).wait_recv())
        flow = ghost_flow(level, in_buf[slot].reshape(ROWS, EL))
        flows[level] = flow
        solve_in[...] = base[...] - flow
        return carry

    lax.fori_loop(0, 2 * LEVELS - 1, level_step, 0)
    advance(0)
    swept_ref[...] = state[...]
    each_peer(lambda s, z: first_arrival(s, z).wait_send())
    for slot in range(2):
        each_peer(lambda s, z: arrival(slot, s, z).wait_send())


def body(
    start_state,
    right_side,
    block_inverse,
    lifted_flux_jacobian,
    face_weight,
    dep_level,
    face_link,
    send_list,
    recv_list,
):
    vmem = pl.BlockSpec(memory_space=pltpu.VMEM)
    out = jax.ShapeDtypeStruct((BLOCK, EL), F32)
    width = 6 * PAD
    return pl.pallas_call(
        kernel,
        out_shape=(out, out),
        in_specs=[vmem, vmem, pl.BlockSpec(memory_space=pl.ANY)] + [vmem] * 6,
        out_specs=(vmem, vmem),
        scratch_shapes=[
            pltpu.VMEM((BLOCK, BLOCK, EL), F32),
            pltpu.VMEM((BLOCK, EL), F32),
            pltpu.VMEM((6, PAD, EL), F32),
            pltpu.VMEM((BLOCK, EL), F32),
            pltpu.VMEM((BLOCK, EL), F32),
            pltpu.VMEM((BLOCK, EL), F32),
            pltpu.VMEM((BLOCK, width), F32),
            pltpu.VMEM((BLOCK, 3 * width), BF16),
            pltpu.VMEM((6, 2 * EL, EL), BF16),
            pltpu.VMEM((LEVELS, ROWS, 6 * EL), BF16),
            pltpu.VMEM((LEVELS, 2 * ROWS, EL), BF16),
            pltpu.VMEM((LEVELS, ROWS, width), F32),
            pltpu.VMEM((LEVELS, BLOCK, EL), F32),
            pltpu.VMEM((ROWS, EL), jnp.int32),
            pltpu.VMEM((2, GROUPS, 8, EL), F32),
            pltpu.VMEM((2, GROUPS, 8, EL), F32),
            pltpu.VMEM((LEVELS, GROUPS, 8, EL), F32),
            pltpu.VMEM((LEVELS, GROUPS, 8, EL), F32),
            pltpu.SemaphoreType.DMA,
            pltpu.SemaphoreType.DMA((2, GROUPS)),
            pltpu.SemaphoreType.DMA((2, GROUPS)),
            pltpu.SemaphoreType.DMA((GROUPS,)),
            pltpu.SemaphoreType.DMA((GROUPS,)),
        ],
        compiler_params=pltpu.CompilerParams(
            collective_id=0, has_side_effects=True, vmem_limit_bytes=60 << 20
        ),
    )(
        start_state,
        right_side,
        block_inverse,
        lifted_flux_jacobian,
        face_weight,
        dep_level.reshape(1, EL),
        face_link,
        send_list,
        recv_list,
    )


def solution(mesh):
    return jax.shard_map(
        body,
        mesh=mesh,
        in_specs=(
            P(None, ("curve", "slab")),
            P(None, ("curve", "slab")),
            P(None, None, ("curve", "slab")),
            P(),
            P(None, ("curve", "slab")),
            P(("curve", "slab")),
            P(None, ("curve", "slab")),
            P(None, ("curve", "slab")),
            P(None, ("curve", "slab")),
        ),
        out_specs=(P(None, ("curve", "slab")), P(None, ("curve", "slab"))),
        check_vma=False,
    )
```

time: 519 us -> 120 us (0.23); the launches traced: 512 us -> 118 us
  starting transfers between devices: 145 us -> 0 us
  local copies, waits for them, and re-layouts: 122 us -> 4.99 us
  Pallas kernels: 0 us -> 113 us
  other arithmetic: 103 us -> 0 us
  blocking collectives: 97.8 us -> 0 us
  waiting for transfers between devices: 27.3 us -> 0 us
  matrix products: 12.3 us -> 0 us
    ppermute x32 -> x0, starting transfers between devices: 140 us -> none  [passed_along(): return lax.ppermute(block, axis, route)]
    pallas_call x0 -> x1, Pallas kernels: none -> 113 us  [body(): pl.pallas_call(kernel, out_shape=(out, out), in_specs=[vmem, vmem, pl.Blo...]
    all_to_all x15 -> x0, blocking collectives: 97.8 us -> none  [route_traces(): lax.all_to_all(nearby, 'slab', split_axis=2, concat_axis=2, tiled=True)]
    dot_general x16 -> x0, other arithmetic: 78.1 us -> none  [advance(): jnp.einsum('ije,je->ie', block_inverse, right_side - flows, precision=lax...]
    gather x32 -> x0, local copies, waits for them, and re-layouts: 51.5 us -> none  [the longest x16 26.3 us: deliver_traces(): arrived = route_traces(traces[:, sends], width)]
    scatter x16 -> x0, local copies, waits for them, and re-layouts: 38.2 us -> none  [deliver_traces(): return ghosts.at[:, recvs].set(arrived)]
    ppermute x32 -> x0, waiting for transfers between devices: 22.8 us -> none  [passed_along(): return lax.ppermute(block, axis, route)]
    dot_general x16 -> x0, matrix products: 12.3 us -> none  [inflow(): jnp.einsum('vuh,hvw->uw', lifted_flux_jacobian, weighted_traces, precisio...]
  transfers between devices with their start and end apart: 33 -> 0, of which waited for: 17 -> 0; matrix products, arithmetic and copies ran while one was open for 0% -> 0% of each run, Pallas kernels for 0% -> 0%
where the time goes in v1:
time: 120 us; the launch traced here: 118 us
  Pallas kernels  113 us (94%)
  local copies, waits for them, and re-layouts  4.99 us (4%)
    pallas_call x1, Pallas kernels, body(): pl.pallas_call(kernel, out_shape=(out, out), in_specs=[vmem, vmem, pl.Blo...  113 us
    unnamed x3, local copies, waits for them, and re-layouts  4.99 us

profile of v1, /device:TPU:7, one launch (start us, length us, event | category | flops | bytes accessed | tf_op | source)
XLA Modules:
  0.0 118.4 jit_solution(7260273449042492190)
XLA Ops:
  0.6 2.0 %copy.11.jac_ref = f32[6,135,45]{2,1,0:T(8,128)} copy(f32[6,135,45]{1,2,0:T(8,128)} %param.12) | data formatting | bytes 291600 | tf_op args[3]
  2.6 112.8 %shard_map.104 = (f32[135,128]{1,0:T(8,128)}, f32[135,128]{1,0:T(8,128)}) custom-call(f32[135,128]{1,0:T(8,128)} %start_ref.1, f32[135,128]{1,0:T(8,128)} %right_ref.1, f32[135,135,128]{2,1,0:T(8,128)} %inverse_hbm.1, f32[6,135,45]{2,1,0:T(8,128)} %copy.11.jac_ref, f32[6,128]{1,0:T(8,128)} %weight_ref.1, s32[1,128]{1,0:T(1,128)} %bitcast.1, ...), custom_call_target="tpu_custom_call" | custom-call | tf_op jit(solution)/shard_map/pallas_call | solution.py:329
  115.4 1.5 %copy.14 = f32[135,128]{1,0:T(8,128)} copy(f32[135,128]{1,0:T(8,128)} %get-tuple-element.4) | data formatting | bytes 138240
  116.9 1.5 %copy.15 = f32[135,128]{1,0:T(8,128)} copy(f32[135,128]{1,0:T(8,128)} %get-tuple-element.5) | data formatting | bytes 138240

commit v2 on v1

--- a/solution.py
+++ b/solution.py
@@ -16,6 +16,7 @@
 PAD = 64
 GROUPS = 12
 ROWS = 8 * GROUPS
+FAR = 32
 MESH = pl.DeviceIdType.MESH
 F32 = jnp.float32
 BF16 = jnp.bfloat16
@@ -58,6 +59,11 @@
     links,
     picks,
     drops,
+    far_drops,
+    far_lane,
+    far_spread,
+    chosen,
+    partial,
     factors,
     flows,
     index,
@@ -75,31 +81,39 @@
     slabs = lax.axis_size("slab")
     my_curve = lax.axis_index("curve")
     my_slab = lax.axis_index("slab")
-    own_group = slabs + my_slab
+    odd = lax.rem(my_curve, 2)
+    far_curve = my_curve + 2 * odd - 1
+    pair_curve = my_curve + 1 - 2 * odd
+    has_far = jnp.logical_and(far_curve >= 0, far_curve < curves)
+    kind_curve = (far_curve, my_curve, pair_curve)
+    far, own, pair = range(3)
+    own_group = own * slabs + my_slab
 
     pull = pltpu.make_async_copy(inverse_hbm, inverse, inverse_sem)
     pull.start()
     in_buf[...] = jnp.zeros_like(in_buf)
     first_in[...] = jnp.zeros_like(first_in)
 
+    def each_far(act):
+        @pl.when(has_far)
+        def _():
+            for shift in (2, 1, 3, 0):
+                act(far, lax.rem(my_slab + shift, slabs))
+
+    def each_near(act):
+        for shift in (2, 1, 3):
+            act(own, lax.rem(my_slab + shift, slabs))
+            act(pair, lax.rem(my_slab + shift, slabs))
+        act(pair, my_slab)
+
     def each_peer(act):
-        @pl.when(my_curve > 0)
-        def _():
-            for z in range(slabs):
-                act(-1, z)
-
-        @pl.when(my_curve < curves - 1)
-        def _():
-            for z in range(slabs):
-                act(1, z)
-
-        for shift in range(1, slabs):
-            act(0, lax.rem(my_slab + shift, slabs))
+        each_far(act)
+        each_near(act)
 
     barrier = pltpu.get_barrier_semaphore()
     each_peer(
-        lambda step, z: pl.semaphore_signal(
-            barrier, inc=1, device_id=(my_curve + step, z), device_id_type=MESH
+        lambda kind, z: pl.semaphore_signal(
+            barrier, inc=1, device_id=(kind_curve[kind], z), device_id_type=MESH
         )
     )
 
@@ -109,9 +123,14 @@
         shift = lax.rem((curves + 1 - my_curve) * (slabs * CAP), curves * slabs * CAP)
         near = pltpu.roll(list_ref[...], shift, 1)[:, :EL]
         tall = jnp.concatenate([near] * 16, axis=0).T
-        index[...] = jnp.full_like(index, 6 * EL)
+        step = slabs * CAP
+        low, mid, high = (tall[step * k : step * (k + 1), :] for k in range(3))
+        ordered = (jnp.where(odd == 1, high, low), mid, jnp.where(odd == 1, low, high))
         for group in range(GROUPS):
-            index[8 * group : 8 * group + CAP, :] = tall[CAP * group : CAP * (group + 1), :]
+            at = CAP * (group % slabs)
+            four = ordered[group // slabs][at : at + CAP, :]
+            index[8 * group : 8 * group + CAP, :] = four
+            index[8 * group + CAP : 8 * group + 8, :] = four
 
     table[...] = jnp.zeros_like(table)
 
@@ -147,64 +166,64 @@
     for level in range(LEVELS):
         first_out[level] = packed(level).reshape(GROUPS, 8, EL)
 
-    @pl.when(jnp.logical_and(my_curve > 0, my_curve < curves - 1))
+    @pl.when(has_far)
     def _():
         pl.semaphore_wait(barrier, 3 * slabs - 1)
 
-    @pl.when(jnp.logical_or(my_curve == 0, my_curve == curves - 1))
+    @pl.when(jnp.logical_not(has_far))
     def _():
         pl.semaphore_wait(barrier, 2 * slabs - 1)
 
-    def first_copy(step, z):
+    def first_copy(kind, z):
         return pltpu.make_async_remote_copy(
-            src_ref=first_out.at[:, (1 + step) * slabs + z],
-            dst_ref=first_in.at[:, (1 - step) * slabs + my_slab],
-            send_sem=first_send_sem.at[(1 + step) * slabs + z],
-            recv_sem=first_recv_sem.at[(1 - step) * slabs + my_slab],
-            device_id=(my_curve + step, z),
+            src_ref=first_out.at[:, kind * slabs + z],
+            dst_ref=first_in.at[:, kind * slabs + my_slab],
+            send_sem=first_send_sem.at[kind * slabs + z],
+            recv_sem=first_recv_sem.at[kind * slabs + my_slab],
+            device_id=(kind_curve[kind], z),
             device_id_type=MESH,
         )
 
-    def first_arrival(step, z):
-        group = (1 + step) * slabs + z
+    def first_arrival(kind, z):
+        group = kind * slabs + z
         return pltpu.make_async_remote_copy(
             src_ref=first_out.at[:, group],
             dst_ref=first_in.at[:, group],
             send_sem=first_send_sem.at[group],
             recv_sem=first_recv_sem.at[group],
-            device_id=(my_curve + step, z),
+            device_id=(kind_curve[kind], z),
             device_id_type=MESH,
         )
 
-    def copy(slot, step, z):
+    def copy(slot, kind, z):
         return pltpu.make_async_remote_copy(
-            src_ref=out_buf.at[slot, (1 + step) * slabs + z],
-            dst_ref=in_buf.at[slot, (1 - step) * slabs + my_slab],
-            send_sem=send_sem.at[slot, (1 + step) * slabs + z],
-            recv_sem=recv_sem.at[slot, (1 - step) * slabs + my_slab],
-            device_id=(my_curve + step, z),
+            src_ref=out_buf.at[slot, kind * slabs + z],
+            dst_ref=in_buf.at[slot, kind * slabs + my_slab],
+            send_sem=send_sem.at[slot, kind * slabs + z],
+            recv_sem=recv_sem.at[slot, kind * slabs + my_slab],
+            device_id=(kind_curve[kind], z),
             device_id_type=MESH,
         )
 
-    def arrival(slot, step, z):
-        group = (1 + step) * slabs + z
+    def arrival(slot, kind, z):
+        group = kind * slabs + z
         return pltpu.make_async_remote_copy(
             src_ref=out_buf.at[slot, group],
             dst_ref=in_buf.at[slot, group],
             send_sem=send_sem.at[slot, group],
             recv_sem=recv_sem.at[slot, group],
-            device_id=(my_curve + step, z),
+            device_id=(kind_curve[kind], z),
             device_id_type=MESH,
         )
 
-    each_peer(lambda step, z: first_copy(step, z).start())
+    each_peer(lambda kind, z: first_copy(kind, z).start())
     first_in[:, own_group] = first_out[:, own_group]
 
     jac[...] = jnp.zeros_like(jac)
     for face in range(6):
-        jac[:, PAD * face : PAD * face + TRACE] = jac_ref[face]
-    jac_hi, jac_lo = split(jac[...])
+        jac[PAD * face : PAD * face + TRACE, :BLOCK] = jac_ref[face]
     width = 6 * PAD
+    jac_hi, jac_lo = split(jac[...].T[:BLOCK])
     jac3[:, :width] = jac_hi
     jac3[:, width : 2 * width] = jac_lo
     jac3[:, 2 * width :] = jac_hi
@@ -217,6 +236,7 @@
 
     to_rows(recv_ref)
     face_lane = lax.broadcasted_iota(jnp.int32, (ROWS, width), 1) // PAD
+    first_half = lax.broadcasted_iota(jnp.int32, (ROWS, EL), 0) % 8 < CAP
     for level in range(LEVELS):
         column = index[:, level : level + 1]
         hit = jnp.zeros((ROWS, EL), F32)
@@ -225,11 +245,11 @@
             mine = column == lane + EL * face
             hit = jnp.where(mine, 1.0, hit)
             gain = jnp.where(mine, weight_ref[face : face + 1, :], gain)
-        one = hit.astype(BF16)
-        drops[level, :ROWS, :] = one
-        drops[level, ROWS:, :] = one
+        drops[level] = jnp.where(first_half, hit, 0.0).astype(BF16)
+        far_drops[level] = jnp.concatenate([hit[:FAR].astype(BF16)] * 4, axis=0)
         scale = jnp.sum(gain, axis=1, keepdims=True)
         factors[level] = jnp.where(column // EL == face_lane, scale, 0.0)
+    far_lane[...] = (jnp.concatenate([index[:FAR, :]] * 4, axis=0).T)[:8] % EL
 
     def local_flow():
         parts_hi = []
@@ -245,26 +265,32 @@
         lo = jnp.concatenate(parts_lo, axis=0)
         return dot(jac3[...], jnp.concatenate([hi, hi, lo], axis=0))
 
-    def ghost_flow(level, block):
-        thrice = jnp.concatenate([block] * 3, axis=1) * factors[level]
-        hi, lo = split(thrice)
-        spread = dot_t(jac3[...], jnp.concatenate([hi, hi, lo], axis=1))
-        hi, lo = split(spread)
-        return dot(jnp.concatenate([hi, lo], axis=1), drops[level])
+    def scattered(values, where_to):
+        hi, lo = split(values)
+        return dot(
+            jnp.concatenate([hi, lo], axis=1), jnp.concatenate([where_to, where_to], axis=0)
+        )
+
+    def spread(block, factor, repeat):
+        hi, lo = split(jnp.concatenate([block] * 3, axis=1) * factor)
+        thrice = jnp.concatenate([hi, hi, lo], axis=1)
+        return dot_t(jac3[...], jnp.concatenate([thrice] * repeat, axis=0))
 
     local = local_flow()
-    each_peer(lambda step, z: first_arrival(step, z).wait_recv())
+    each_peer(lambda kind, z: first_arrival(kind, z).wait_recv())
     known = right_ref[...] - local
     for level in range(LEVELS):
-        flow = ghost_flow(level, first_in[level].reshape(ROWS, EL))
+        flow = scattered(
+            spread(first_in[level].reshape(ROWS, EL), factors[level], 1), drops[level]
+        )
         flows[level] = flow
         known = known - flow
     solve_in[...] = known
     pull.wait()
 
-    chunk = 9
-
-    def advance(level):
+    chunk = 27
+
+    def multiply():
         vector = solve_in[...]
 
         def rows(at, carry):
@@ -274,12 +300,68 @@
             return carry
 
         lax.fori_loop(0, BLOCK // chunk, rows, 0)
-        state[...] = jnp.where(level_ref[...] == level, update[...], state[...])
+
+    lanes8 = lax.broadcasted_iota(jnp.int32, (8, EL), 1)
+    part_of = (lanes8 // 32) * 2 + (lanes8 // 4) % 2
+    tail = lax.broadcasted_iota(jnp.int32, (8, EL), 0) < BLOCK - 128
+
+    def choose(level):
+        where_from = jnp.broadcast_to(far_lane[pl.ds(level, 1), :], (8, EL))
+
+        def rows_one(i, carry):
+            for half in range(2):
+                got = None
+                for part in range(8):
+                    at = 64 * half + 8 * part
+                    moved = jnp.take_along_axis(inverse[i, at : at + 8, :], where_from, axis=1)
+                    got = moved if got is None else jnp.where(part_of == part, moved, got)
+                chosen[i, 8 * half : 8 * half + 8, :] = got
+            last = jnp.concatenate(
+                [inverse[i, 128:BLOCK, :], jnp.zeros((136 - BLOCK, EL), F32)], axis=0
+            )
+            chosen[i, 16:24, :] = jnp.where(
+                tail, jnp.take_along_axis(last, where_from, axis=1), 0.0
+            )
+            return carry
+
+        def rows(at, carry):
+            for k in range(27):
+                rows_one(at * 27 + k, carry)
+            return carry
+
+        lax.fori_loop(0, BLOCK // 27, rows, 0)
+
+    def fold(values):
+        pieces = []
+        for half in range(2):
+            got = None
+            for part in range(8):
+                at = 64 * half + 8 * part
+                piece = values[at : at + 8]
+                got = piece if got is None else jnp.where(part_of == part, piece, got)
+            pieces.append(got)
+        last = jnp.concatenate([values[128:BLOCK], jnp.zeros((136 - BLOCK, EL), F32)], axis=0)
+        pieces.append(jnp.where(part_of == 0, last, 0.0))
+        return jnp.concatenate(pieces, axis=0)
+
+    def level_of(step):
+        return jnp.where(step < LEVELS, step, 2 * LEVELS - 1 - step)
+
+    def far_multiply(vector):
+        def rows(at, carry):
+            for k in range(chunk):
+                i = at * chunk + k
+                partial[pl.ds(i, 1), :] = jnp.sum(chosen[i] * vector, axis=0, keepdims=True)
+            return carry
+
+        lax.fori_loop(0, BLOCK // chunk, rows, 0)
+
+    multiply()
+    state[...] = jnp.where(level_ref[...] == 0, update[...], state[...])
 
     def level_step(step, carry):
-        level = jnp.where(step < LEVELS, step, 2 * LEVELS - 1 - step)
+        level = level_of(step)
         slot = lax.rem(step, 2)
-        advance(level)
 
         @pl.when(step >= 2)
         def _():
@@ -294,18 +376,34 @@
         def _():
             forward_ref[...] = state[...]
 
+        @pl.when(step > 0)
+        def _():
+            before = level_of(step - 1)
+            flows[before] = flows[before] + scattered(
+                jnp.where(part_of[:1] == 0, far_spread[...], 0.0), far_drops[before]
+            )
+
         known = right_ref[...] - local_flow()
         for other in range(LEVELS):
             known = known - jnp.where(level == other, 0.0, flows[other])
         base[...] = known
-        each_peer(lambda s, z: arrival(slot, s, z).wait_recv())
-        flow = ghost_flow(level, in_buf[slot].reshape(ROWS, EL))
+        choose(level)
+        each_near(lambda s, z: arrival(slot, s, z).wait_recv())
+        block = in_buf[slot, slabs:].reshape(ROWS - FAR, EL)
+        flow = scattered(spread(block, factors[level, FAR:], 1), drops[level, FAR:])
         flows[level] = flow
         solve_in[...] = base[...] - flow
+        multiply()
+        each_far(lambda s, z: arrival(slot, s, z).wait_recv())
+        block = in_buf[slot, :slabs].reshape(FAR, EL)
+        far_values = spread(block, factors[level, :FAR], 4)
+        far_spread[...] = far_values
+        far_multiply(fold(far_values))
+        fresh = update[...] - scattered(partial[...], far_drops[level])
+        state[...] = jnp.where(level_ref[...] == level_of(step + 1), fresh, state[...])
         return carry
 
     lax.fori_loop(0, 2 * LEVELS - 1, level_step, 0)
-    advance(0)
     swept_ref[...] = state[...]
     each_peer(lambda s, z: first_arrival(s, z).wait_send())
     for slot in range(2):
@@ -338,11 +436,16 @@
             pltpu.VMEM((BLOCK, EL), F32),
             pltpu.VMEM((BLOCK, EL), F32),
             pltpu.VMEM((BLOCK, EL), F32),
-            pltpu.VMEM((BLOCK, width), F32),
+            pltpu.VMEM((width, 256), F32),
             pltpu.VMEM((BLOCK, 3 * width), BF16),
             pltpu.VMEM((6, 2 * EL, EL), BF16),
             pltpu.VMEM((LEVELS, ROWS, 6 * EL), BF16),
-            pltpu.VMEM((LEVELS, 2 * ROWS, EL), BF16),
+            pltpu.VMEM((LEVELS, ROWS, EL), BF16),
+            pltpu.VMEM((LEVELS, EL, EL), BF16),
+            pltpu.VMEM((8, EL), jnp.int32),
+            pltpu.VMEM((BLOCK, EL), F32),
+            pltpu.VMEM((BLOCK, 24, EL), F32),
+            pltpu.VMEM((BLOCK, EL), F32),
             pltpu.VMEM((LEVELS, ROWS, width), F32),
             pltpu.VMEM((LEVELS, BLOCK, EL), F32),
             pltpu.VMEM((ROWS, EL), jnp.int32),
@@ -363,7 +466,7 @@
         start_state,
         right_side,
         block_inverse,
-        lifted_flux_jacobian,
+        lifted_flux_jacobian.swapaxes(1, 2),
         face_weight,
         dep_level.reshape(1, EL),
         face_link,

time: 120 us -> 109 us (0.908); the launches traced: 118 us -> 109 us
  Pallas kernels: 113 us -> 105 us
  local copies, waits for them, and re-layouts: 4.99 us -> 3.04 us
    pallas_call x1, Pallas kernels: 113 us -> 105 us  [body(): pl.pallas_call(kernel, out_shape=(out, out), in_specs=[vmem, vmem, pl.Blo...]
    unnamed x3 -> x2, local copies, waits for them, and re-layouts: 4.99 us -> 3.04 us
where the time goes in v2:
time: 109 us
  Pallas kernels  105 us (96%)
  local copies, waits for them, and re-layouts  3.04 us (3%)
    pallas_call x1, Pallas kernels, body(): pl.pallas_call(kernel, out_shape=(out, out), in_specs=[vmem, vmem, pl.Blo...  105 us
    unnamed x2, local copies, waits for them, and re-layouts  3.04 us

profile of v2, /device:TPU:7, one launch (start us, length us, event | category | flops | bytes accessed | tf_op | source)
XLA Modules:
  0.0 109.0 jit_solution(10128930531770163991)
XLA Ops:
  0.6 105.3 %shard_map.104 = (f32[135,128]{1,0:T(8,128)}, f32[135,128]{1,0:T(8,128)}) custom-call(f32[135,128]{1,0:T(8,128)} %start_ref.1, f32[135,128]{1,0:T(8,128)} %right_ref.1, f32[135,135,128]{2,1,0:T(8,128)} %inverse_hbm.1, f32[6,45,135]{2,1,0:T(8,128)} %bitcast.2, f32[6,128]{1,0:T(8,128)} %weight_ref.1, s32[1,128]{1,0:T(1,128)} %bitcast.3, s32[6,128]{1,0:T(8,128)} %link_ref.1, ...), custom_call_target="tpu_custom_call" | custom-call | tf_op jit(solution)/shard_map/pallas_call | solution.py:427
  106.0 1.5 %copy.13 = f32[135,128]{1,0:T(8,128)} copy(f32[135,128]{1,0:T(8,128)} %get-tuple-element.4) | data formatting | bytes 138240
  107.5 1.5 %copy.14 = f32[135,128]{1,0:T(8,128)} copy(f32[135,128]{1,0:T(8,128)} %get-tuple-element.5) | data formatting | bytes 138240

commit v3 on v2

--- a/solution.py
+++ b/solution.py
@@ -37,22 +37,28 @@
 
 
 def kernel(
-    start_ref,
+    start_hbm,
+    right_hbm,
+    inverse_hbm,
+    jac_hbm,
+    weight_hbm,
+    level_hbm,
+    link_hbm,
+    send_hbm,
+    recv_hbm,
+    forward_ref,
+    swept_ref,
     right_ref,
-    inverse_hbm,
     jac_ref,
     weight_ref,
     level_ref,
     link_ref,
     send_ref,
     recv_ref,
-    forward_ref,
-    swept_ref,
     inverse,
     state,
     table,
     solve_in,
-    base,
     update,
     jac,
     jac3,
@@ -61,17 +67,19 @@
     drops,
     far_drops,
     far_lane,
+    near_flow,
     far_spread,
-    chosen,
-    partial,
+    far_chosen,
+    far_part,
     factors,
     flows,
+    others,
     index,
     out_buf,
     in_buf,
     first_out,
     first_in,
-    inverse_sem,
+    input_sems,
     send_sem,
     recv_sem,
     first_send_sem,
@@ -89,10 +97,29 @@
     far, own, pair = range(3)
     own_group = own * slabs + my_slab
 
-    pull = pltpu.make_async_copy(inverse_hbm, inverse, inverse_sem)
-    pull.start()
-    in_buf[...] = jnp.zeros_like(in_buf)
-    first_in[...] = jnp.zeros_like(first_in)
+    pulls = [
+        pltpu.make_async_copy(source, target, input_sems.at[at])
+        for at, (source, target) in enumerate(
+            (
+                (start_hbm, state),
+                (send_hbm, send_ref),
+                (recv_hbm, recv_ref),
+                (jac_hbm, jac_ref),
+                (weight_hbm, weight_ref),
+                (link_hbm, link_ref),
+                (right_hbm, right_ref),
+                (level_hbm, level_ref),
+                (inverse_hbm, inverse),
+            )
+        )
+    ]
+    for pull in pulls:
+        pull.start()
+
+    @pl.when(jnp.logical_not(has_far))
+    def _():
+        in_buf[:, :slabs] = jnp.zeros((2, slabs, 8, EL), F32)
+        first_in[:, :slabs] = jnp.zeros((LEVELS, slabs, 8, EL), F32)
 
     def each_far(act):
         @pl.when(has_far)
@@ -146,7 +173,8 @@
                 ]
             table[4 + side, :TRACE, :] = state[pl.ds(2 * side, TRACE, stride=3), :]
 
-    state[...] = start_ref[...]
+    for pull in pulls[:2]:
+        pull.wait()
     fill_table()
     to_rows(send_ref)
     for level in range(LEVELS):
@@ -219,6 +247,8 @@
     each_peer(lambda kind, z: first_copy(kind, z).start())
     first_in[:, own_group] = first_out[:, own_group]
 
+    for pull in pulls[2:8]:
+        pull.wait()
     jac[...] = jnp.zeros_like(jac)
     for face in range(6):
         jac[PAD * face : PAD * face + TRACE, :BLOCK] = jac_ref[face]
@@ -276,17 +306,20 @@
         thrice = jnp.concatenate([hi, hi, lo], axis=1)
         return dot_t(jac3[...], jnp.concatenate([thrice] * repeat, axis=0))
 
-    local = local_flow()
-    each_peer(lambda kind, z: first_arrival(kind, z).wait_recv())
-    known = right_ref[...] - local
-    for level in range(LEVELS):
-        flow = scattered(
-            spread(first_in[level].reshape(ROWS, EL), factors[level], 1), drops[level]
-        )
-        flows[level] = flow
-        known = known - flow
-    solve_in[...] = known
-    pull.wait()
+    def first_flow(low, high):
+        count = LEVELS * (high - low) * 8
+        block = first_in[:, low:high].reshape(count, EL)
+        values = spread(block, factors[:, 8 * low : 8 * high].reshape(count, width), 1)
+        return scattered(values, drops[:, 8 * low : 8 * high].reshape(count, EL))
+
+    known = right_ref[...] - local_flow()
+    each_near(lambda kind, z: first_arrival(kind, z).wait_recv())
+    ghost = first_flow(slabs, GROUPS)
+    each_far(lambda kind, z: first_arrival(kind, z).wait_recv())
+    ghost = ghost + first_flow(0, slabs)
+    others[...] = ghost
+    solve_in[...] = known - ghost
+    pulls[8].wait()
 
     chunk = 27
 
@@ -302,59 +335,65 @@
         lax.fori_loop(0, BLOCK // chunk, rows, 0)
 
     lanes8 = lax.broadcasted_iota(jnp.int32, (8, EL), 1)
-    part_of = (lanes8 // 32) * 2 + (lanes8 // 4) % 2
+    second = (lanes8 // 4) % 2
+    far_place = (lanes8 // 32) * 2 + second
     tail = lax.broadcasted_iota(jnp.int32, (8, EL), 0) < BLOCK - 128
 
+    def merged(pieces, place):
+        got = pieces[0]
+        for part in range(1, len(pieces)):
+            got = jnp.where(place == part, pieces[part], got)
+        return got
+
+    def tail_of(values):
+        return jnp.concatenate([values, jnp.zeros((136 - BLOCK, EL), F32)], axis=0)
+
     def choose(level):
-        where_from = jnp.broadcast_to(far_lane[pl.ds(level, 1), :], (8, EL))
-
-        def rows_one(i, carry):
-            for half in range(2):
-                got = None
-                for part in range(8):
-                    at = 64 * half + 8 * part
-                    moved = jnp.take_along_axis(inverse[i, at : at + 8, :], where_from, axis=1)
-                    got = moved if got is None else jnp.where(part_of == part, moved, got)
-                chosen[i, 8 * half : 8 * half + 8, :] = got
-            last = jnp.concatenate(
-                [inverse[i, 128:BLOCK, :], jnp.zeros((136 - BLOCK, EL), F32)], axis=0
+        far_from = jnp.broadcast_to(far_lane[pl.ds(level, 1), :], (8, EL))
+
+        def row_of(i, target, where_from, place, parts):
+            for m in range(16 // parts):
+                pieces = [
+                    jnp.take_along_axis(
+                        inverse[i, 8 * (m * parts + part) : 8 * (m * parts + part + 1), :],
+                        where_from,
+                        axis=1,
+                    )
+                    for part in range(parts)
+                ]
+                target[i, 8 * m : 8 * m + 8, :] = merged(pieces, place)
+            last = jnp.take_along_axis(tail_of(inverse[i, 128:BLOCK, :]), where_from, axis=1)
+            at = 128 // parts
+            target[i, at : at + 8, :] = jnp.where(tail, last, 0.0)
+
+        def far_rows(at, carry):
+            for k in range(chunk):
+                row_of(at * chunk + k, far_chosen, far_from, far_place, 8)
+            return carry
+
+        lax.fori_loop(0, BLOCK // chunk, far_rows, 0)
+
+    def fold(values, place, parts):
+        pieces = []
+        for m in range(16 // parts):
+            at = 8 * parts * m
+            pieces.append(
+                merged([values[at + 8 * p : at + 8 * p + 8] for p in range(parts)], place)
             )
-            chosen[i, 16:24, :] = jnp.where(
-                tail, jnp.take_along_axis(last, where_from, axis=1), 0.0
-            )
-            return carry
-
-        def rows(at, carry):
-            for k in range(27):
-                rows_one(at * 27 + k, carry)
-            return carry
-
-        lax.fori_loop(0, BLOCK // 27, rows, 0)
-
-    def fold(values):
-        pieces = []
-        for half in range(2):
-            got = None
-            for part in range(8):
-                at = 64 * half + 8 * part
-                piece = values[at : at + 8]
-                got = piece if got is None else jnp.where(part_of == part, piece, got)
-            pieces.append(got)
-        last = jnp.concatenate([values[128:BLOCK], jnp.zeros((136 - BLOCK, EL), F32)], axis=0)
-        pieces.append(jnp.where(part_of == 0, last, 0.0))
+        pieces.append(jnp.where(place == 0, tail_of(values[128:BLOCK]), 0.0))
         return jnp.concatenate(pieces, axis=0)
 
-    def level_of(step):
-        return jnp.where(step < LEVELS, step, 2 * LEVELS - 1 - step)
-
-    def far_multiply(vector):
+    def part_multiply(chosen, vector, target):
         def rows(at, carry):
             for k in range(chunk):
                 i = at * chunk + k
-                partial[pl.ds(i, 1), :] = jnp.sum(chosen[i] * vector, axis=0, keepdims=True)
+                target[pl.ds(i, 1), :] = jnp.sum(chosen[i] * vector, axis=0, keepdims=True)
             return carry
 
         lax.fori_loop(0, BLOCK // chunk, rows, 0)
+
+    def level_of(step):
+        return jnp.where(step < LEVELS, step, 2 * LEVELS - 1 - step)
 
     multiply()
     state[...] = jnp.where(level_ref[...] == 0, update[...], state[...])
@@ -379,27 +418,33 @@
         @pl.when(step > 0)
         def _():
             before = level_of(step - 1)
-            flows[before] = flows[before] + scattered(
-                jnp.where(part_of[:1] == 0, far_spread[...], 0.0), far_drops[before]
+            flow = near_flow[...] + scattered(
+                jnp.where(far_place[:1] == 0, far_spread[...], 0.0), far_drops[before]
             )
-
-        known = right_ref[...] - local_flow()
-        for other in range(LEVELS):
-            known = known - jnp.where(level == other, 0.0, flows[other])
-        base[...] = known
+            flows[before] = flow
+            others[...] = others[...] + flow
+
+        @pl.when(step < LEVELS)
+        def _():
+            block = first_in[level].reshape(ROWS, EL)
+            flows[level] = scattered(spread(block, factors[level], 1), drops[level])
+
+        rest = others[...] - flows[level]
+        others[...] = rest
+        solve_in[...] = right_ref[...] - local_flow() - rest
         choose(level)
         each_near(lambda s, z: arrival(slot, s, z).wait_recv())
         block = in_buf[slot, slabs:].reshape(ROWS - FAR, EL)
         flow = scattered(spread(block, factors[level, FAR:], 1), drops[level, FAR:])
-        flows[level] = flow
-        solve_in[...] = base[...] - flow
+        near_flow[...] = flow
+        solve_in[...] = solve_in[...] - flow
         multiply()
         each_far(lambda s, z: arrival(slot, s, z).wait_recv())
         block = in_buf[slot, :slabs].reshape(FAR, EL)
-        far_values = spread(block, factors[level, :FAR], 4)
-        far_spread[...] = far_values
-        far_multiply(fold(far_values))
-        fresh = update[...] - scattered(partial[...], far_drops[level])
+        values = spread(block, factors[level, :FAR], 4)
+        far_spread[...] = values
+        part_multiply(far_chosen, fold(values, far_place, 8), far_part)
+        fresh = update[...] - scattered(far_part[...], far_drops[level])
         state[...] = jnp.where(level_ref[...] == level_of(step + 1), fresh, state[...])
         return carry
 
@@ -408,6 +453,17 @@
     each_peer(lambda s, z: first_arrival(s, z).wait_send())
     for slot in range(2):
         each_peer(lambda s, z: arrival(slot, s, z).wait_send())
+
+
+def hand_on(first_ref, second_ref, first_out, second_out, sems):
+    copies = (
+        pltpu.make_async_copy(first_ref, first_out, sems.at[0]),
+        pltpu.make_async_copy(second_ref, second_out, sems.at[1]),
+    )
+    for one in copies:
+        one.start()
+    for one in copies:
+        one.wait()
 
 
 def body(
@@ -424,16 +480,24 @@
     vmem = pl.BlockSpec(memory_space=pltpu.VMEM)
     out = jax.ShapeDtypeStruct((BLOCK, EL), F32)
     width = 6 * PAD
-    return pl.pallas_call(
+    lists = send_list.shape[1]
+    hbm = pl.BlockSpec(memory_space=pl.ANY)
+    first, second = pl.pallas_call(
         kernel,
         out_shape=(out, out),
-        in_specs=[vmem, vmem, pl.BlockSpec(memory_space=pl.ANY)] + [vmem] * 6,
+        in_specs=[hbm] * 9,
         out_specs=(vmem, vmem),
         scratch_shapes=[
+            pltpu.VMEM((BLOCK, EL), F32),
+            pltpu.VMEM((6, TRACE, BLOCK), F32),
+            pltpu.VMEM((6, EL), F32),
+            pltpu.VMEM((1, EL), jnp.int32),
+            pltpu.VMEM((6, EL), jnp.int32),
+            pltpu.VMEM((LEVELS, lists), jnp.int32),
+            pltpu.VMEM((LEVELS, lists), jnp.int32),
             pltpu.VMEM((BLOCK, BLOCK, EL), F32),
             pltpu.VMEM((BLOCK, EL), F32),
             pltpu.VMEM((6, PAD, EL), F32),
-            pltpu.VMEM((BLOCK, EL), F32),
             pltpu.VMEM((BLOCK, EL), F32),
             pltpu.VMEM((BLOCK, EL), F32),
             pltpu.VMEM((width, 256), F32),
@@ -444,16 +508,18 @@
             pltpu.VMEM((LEVELS, EL, EL), BF16),
             pltpu.VMEM((8, EL), jnp.int32),
             pltpu.VMEM((BLOCK, EL), F32),
+            pltpu.VMEM((BLOCK, EL), F32),
             pltpu.VMEM((BLOCK, 24, EL), F32),
             pltpu.VMEM((BLOCK, EL), F32),
             pltpu.VMEM((LEVELS, ROWS, width), F32),
             pltpu.VMEM((LEVELS, BLOCK, EL), F32),
+            pltpu.VMEM((BLOCK, EL), F32),
             pltpu.VMEM((ROWS, EL), jnp.int32),
             pltpu.VMEM((2, GROUPS, 8, EL), F32),
             pltpu.VMEM((2, GROUPS, 8, EL), F32),
             pltpu.VMEM((LEVELS, GROUPS, 8, EL), F32),
             pltpu.VMEM((LEVELS, GROUPS, 8, EL), F32),
-            pltpu.SemaphoreType.DMA,
+            pltpu.SemaphoreType.DMA((9,)),
             pltpu.SemaphoreType.DMA((2, GROUPS)),
             pltpu.SemaphoreType.DMA((2, GROUPS)),
             pltpu.SemaphoreType.DMA((GROUPS,)),
@@ -473,6 +539,13 @@
         send_list,
         recv_list,
     )
+    return pl.pallas_call(
+        hand_on,
+        out_shape=(out, out),
+        in_specs=[vmem, vmem],
+        out_specs=(hbm, hbm),
+        scratch_shapes=[pltpu.SemaphoreType.DMA((2,))],
+    )(first, second)
 
 
 def solution(mesh):

time: 109 us -> 109 us (level)
  local copies, waits for them, and re-layouts: 3.04 us -> 0 us
  Pallas kernels: 105 us -> 108 us
    unnamed x2 -> x0, local copies, waits for them, and re-layouts: 3.04 us -> none
    pallas_call x1 -> x2, Pallas kernels: 105 us -> 108 us  [the longest x1 106 us: body(): pl.pallas_call(kernel, out_shape=(out, out), in_specs=[hbm] * 9, out_spec...]
where the time goes in v3:
time: 109 us
  Pallas kernels  108 us (99%)
    pallas_call x1, Pallas kernels, body(): pl.pallas_call(kernel, out_shape=(out, out), in_specs=[hbm] * 9, out_spec...  106 us

profile of v3, /device:TPU:7, one launch (start us, length us, event | category | flops | bytes accessed | tf_op | source)
XLA Modules:
  0.0 108.6 jit_solution(8845384488087174356)
XLA Ops:
  0.6 106.4 %shard_map.104 = (f32[135,128]{1,0:T(8,128)}, f32[135,128]{1,0:T(8,128)}) custom-call(f32[135,128]{1,0:T(8,128)} %start_hbm.1, f32[135,128]{1,0:T(8,128)} %right_hbm.1, f32[135,135,128]{2,1,0:T(8,128)} %inverse_hbm.1, f32[6,45,135]{2,1,0:T(8,128)} %bitcast.2, f32[6,128]{1,0:T(8,128)} %weight_hbm.1, s32[1,128]{1,0:T(1,128)} %bitcast.3, s32[6,128]{1,0:T(8,128)} %link_hbm.1, ...), custom_call_target="tpu_custom_call" | custom-call | tf_op jit(solution)/shard_map/pallas_call | solution.py:485
  107.0 1.6 %shard_map.105 = (f32[135,128]{1,0:T(8,128)}, f32[135,128]{1,0:T(8,128)}) custom-call(f32[135,128]{1,0:T(8,128)} %get-tuple-element.4.first_ref, f32[135,128]{1,0:T(8,128)} %get-tuple-element.5.second_ref), custom_call_target="tpu_custom_call" | custom-call | tf_op jit(solution)/shard_map/pallas_call | solution.py:542

commit v4 on v3

--- a/solution.py
+++ b/solution.py
@@ -16,7 +16,11 @@
 PAD = 64
 GROUPS = 12
 ROWS = 8 * GROUPS
-FAR = 32
+FAR, OWN, PAIR = range(3)
+LATE = ((FAR, 2), (FAR, 1), (FAR, 3), (FAR, 0), (OWN, 2), (PAIR, 2))
+EARLY = ((OWN, 1), (OWN, 3), (PAIR, 1), (PAIR, 3), (PAIR, 0), (OWN, 0))
+PLACES = {key: at for at, key in enumerate(LATE + EARLY)}
+HALF = 8 * len(LATE)
 MESH = pl.DeviceIdType.MESH
 F32 = jnp.float32
 BF16 = jnp.bfloat16
@@ -65,15 +69,14 @@
     links,
     picks,
     drops,
-    far_drops,
-    far_lane,
-    near_flow,
-    far_spread,
-    far_chosen,
-    far_part,
+    late_drops,
+    late_lane,
+    early_flow,
+    late_spread,
+    late_chosen,
+    late_part,
     factors,
-    flows,
-    others,
+    total,
     index,
     out_buf,
     in_buf,
@@ -94,8 +97,7 @@
     pair_curve = my_curve + 1 - 2 * odd
     has_far = jnp.logical_and(far_curve >= 0, far_curve < curves)
     kind_curve = (far_curve, my_curve, pair_curve)
-    far, own, pair = range(3)
-    own_group = own * slabs + my_slab
+    here = PLACES[OWN, 0]
 
     pulls = [
         pltpu.make_async_copy(source, target, input_sems.at[at])
@@ -118,29 +120,33 @@
 
     @pl.when(jnp.logical_not(has_far))
     def _():
-        in_buf[:, :slabs] = jnp.zeros((2, slabs, 8, EL), F32)
-        first_in[:, :slabs] = jnp.zeros((LEVELS, slabs, 8, EL), F32)
-
-    def each_far(act):
+        in_buf[:, :4] = jnp.zeros((2, 4, 8, EL), F32)
+        first_in[:, :4] = jnp.zeros((LEVELS, 4, 8, EL), F32)
+
+    def each_late(act):
         @pl.when(has_far)
         def _():
-            for shift in (2, 1, 3, 0):
-                act(far, lax.rem(my_slab + shift, slabs))
-
-    def each_near(act):
-        for shift in (2, 1, 3):
-            act(own, lax.rem(my_slab + shift, slabs))
-            act(pair, lax.rem(my_slab + shift, slabs))
-        act(pair, my_slab)
+            for kind, shift in LATE[:4]:
+                act(kind, shift)
+
+        for kind, shift in LATE[4:]:
+            act(kind, shift)
+
+    def each_early(act):
+        for kind, shift in EARLY[:-1]:
+            act(kind, shift)
 
     def each_peer(act):
-        each_far(act)
-        each_near(act)
+        each_late(act)
+        each_early(act)
+
+    def device(kind, shift):
+        return (kind_curve[kind], lax.rem(my_slab + shift, slabs))
 
     barrier = pltpu.get_barrier_semaphore()
     each_peer(
-        lambda kind, z: pl.semaphore_signal(
-            barrier, inc=1, device_id=(kind_curve[kind], z), device_id_type=MESH
+        lambda kind, shift: pl.semaphore_signal(
+            barrier, inc=1, device_id=device(kind, shift), device_id_type=MESH
         )
     )
 
@@ -153,11 +159,17 @@
         step = slabs * CAP
         low, mid, high = (tall[step * k : step * (k + 1), :] for k in range(3))
         ordered = (jnp.where(odd == 1, high, low), mid, jnp.where(odd == 1, low, high))
-        for group in range(GROUPS):
-            at = CAP * (group % slabs)
-            four = ordered[group // slabs][at : at + CAP, :]
-            index[8 * group : 8 * group + CAP, :] = four
-            index[8 * group + CAP : 8 * group + 8, :] = four
+        for kind in range(3):
+            block = ordered[kind]
+            turned = block
+            for z in range(1, slabs):
+                other = jnp.concatenate([block[CAP * z :], block[: CAP * z]], axis=0)
+                turned = jnp.where(my_slab == z, other, turned)
+            for shift in range(slabs):
+                group = PLACES[kind, shift]
+                four = turned[CAP * shift : CAP * (shift + 1), :]
+                index[8 * group : 8 * group + CAP, :] = four
+                index[8 * group + CAP : 8 * group + 8, :] = four
 
     table[...] = jnp.zeros_like(table)
 
@@ -202,50 +214,54 @@
     def _():
         pl.semaphore_wait(barrier, 2 * slabs - 1)
 
-    def first_copy(kind, z):
+    def first_copy(kind, shift):
+        source = PLACES[kind, shift]
+        target = PLACES[kind, (4 - shift) % 4]
         return pltpu.make_async_remote_copy(
-            src_ref=first_out.at[:, kind * slabs + z],
-            dst_ref=first_in.at[:, kind * slabs + my_slab],
-            send_sem=first_send_sem.at[kind * slabs + z],
-            recv_sem=first_recv_sem.at[kind * slabs + my_slab],
-            device_id=(kind_curve[kind], z),
+            src_ref=first_out.at[:, source],
+            dst_ref=first_in.at[:, target],
+            send_sem=first_send_sem.at[source],
+            recv_sem=first_recv_sem.at[target],
+            device_id=device(kind, shift),
             device_id_type=MESH,
         )
 
-    def first_arrival(kind, z):
-        group = kind * slabs + z
+    def first_arrival(kind, shift):
+        place = PLACES[kind, shift]
         return pltpu.make_async_remote_copy(
-            src_ref=first_out.at[:, group],
-            dst_ref=first_in.at[:, group],
-            send_sem=first_send_sem.at[group],
-            recv_sem=first_recv_sem.at[group],
-            device_id=(kind_curve[kind], z),
+            src_ref=first_out.at[:, place],
+            dst_ref=first_in.at[:, place],
+            send_sem=first_send_sem.at[place],
+            recv_sem=first_recv_sem.at[place],
+            device_id=device(kind, shift),
             device_id_type=MESH,
         )
 
-    def copy(slot, kind, z):
+    def copy(slot, kind, shift):
+        source = PLACES[kind, shift]
+        target = PLACES[kind, (4 - shift) % 4]
         return pltpu.make_async_remote_copy(
-            src_ref=out_buf.at[slot, kind * slabs + z],
-            dst_ref=in_buf.at[slot, kind * slabs + my_slab],
-            send_sem=send_sem.at[slot, kind * slabs + z],
-            recv_sem=recv_sem.at[slot, kind * slabs + my_slab],
-            device_id=(kind_curve[kind], z),
+            src_ref=out_buf.at[slot, source],
+            dst_ref=in_buf.at[slot, target],
+            send_sem=send_sem.at[slot, source],
+            recv_sem=recv_sem.at[slot, target],
+            device_id=device(kind, shift),
             device_id_type=MESH,
         )
 
-    def arrival(slot, kind, z):
-        group = kind * slabs + z
+    def arrival(slot, kind, shift):
+        place = PLACES[kind, shift]
         return pltpu.make_async_remote_copy(
-            src_ref=out_buf.at[slot, group],
-            dst_ref=in_buf.at[slot, group],
-            send_sem=send_sem.at[slot, group],
-            recv_sem=recv_sem.at[slot, group],
-            device_id=(kind_curve[kind], z),
+            src_ref=out_buf.at[slot, place],
+            dst_ref=in_buf.at[slot, place],
+            send_sem=send_sem.at[slot, place],
+            recv_sem=recv_sem.at[slot, place],
+            device_id=device(kind, shift),
             device_id_type=MESH,
         )
 
-    each_peer(lambda kind, z: first_copy(kind, z).start())
-    first_in[:, own_group] = first_out[:, own_group]
+    each_peer(lambda kind, shift: first_copy(kind, shift).start())
+    first_in[:, here] = first_out[:, here]
 
     for pull in pulls[2:8]:
         pull.wait()
@@ -263,6 +279,14 @@
         one = jnp.where(link_ref[face : face + 1, :] == row, 1.0, 0.0).astype(BF16)
         links[face, :EL, :] = one
         links[face, EL:, :] = one
+
+    def tiled(rows):
+        low = lax.broadcasted_iota(jnp.int32, (8, rows.shape[1]), 0) < CAP
+        mixed = [
+            jnp.where(low, rows[16 * k : 16 * k + 8], rows[16 * k + 8 : 16 * k + 16])
+            for k in range(3)
+        ]
+        return jnp.concatenate([rows, rows, *mixed, jnp.zeros_like(mixed[0])], axis=0)
 
     to_rows(recv_ref)
     face_lane = lax.broadcasted_iota(jnp.int32, (ROWS, width), 1) // PAD
@@ -276,10 +300,10 @@
             hit = jnp.where(mine, 1.0, hit)
             gain = jnp.where(mine, weight_ref[face : face + 1, :], gain)
         drops[level] = jnp.where(first_half, hit, 0.0).astype(BF16)
-        far_drops[level] = jnp.concatenate([hit[:FAR].astype(BF16)] * 4, axis=0)
+        late_drops[level] = tiled(hit[:HALF]).astype(BF16)
         scale = jnp.sum(gain, axis=1, keepdims=True)
         factors[level] = jnp.where(column // EL == face_lane, scale, 0.0)
-    far_lane[...] = (jnp.concatenate([index[:FAR, :]] * 4, axis=0).T)[:8] % EL
+    late_lane[...] = (tiled(index[:HALF, :]).T)[:8] % EL
 
     def local_flow():
         parts_hi = []
@@ -301,24 +325,24 @@
             jnp.concatenate([hi, lo], axis=1), jnp.concatenate([where_to, where_to], axis=0)
         )
 
-    def spread(block, factor, repeat):
-        hi, lo = split(jnp.concatenate([block] * 3, axis=1) * factor)
-        thrice = jnp.concatenate([hi, hi, lo], axis=1)
-        return dot_t(jac3[...], jnp.concatenate([thrice] * repeat, axis=0))
+    def spread(block, factor, tile=lambda rows: rows):
+        hi, lo = split(tile(jnp.concatenate([block] * 3, axis=1) * factor))
+        return dot_t(jac3[...], jnp.concatenate([hi, hi, lo], axis=1))
 
     def first_flow(low, high):
         count = LEVELS * (high - low) * 8
         block = first_in[:, low:high].reshape(count, EL)
-        values = spread(block, factors[:, 8 * low : 8 * high].reshape(count, width), 1)
+        values = spread(block, factors[:, 8 * low : 8 * high].reshape(count, width))
         return scattered(values, drops[:, 8 * low : 8 * high].reshape(count, EL))
 
     known = right_ref[...] - local_flow()
-    each_near(lambda kind, z: first_arrival(kind, z).wait_recv())
-    ghost = first_flow(slabs, GROUPS)
-    each_far(lambda kind, z: first_arrival(kind, z).wait_recv())
-    ghost = ghost + first_flow(0, slabs)
-    others[...] = ghost
+    each_early(lambda kind, shift: first_arrival(kind, shift).wait_recv())
+    ghost = first_flow(len(LATE), GROUPS)
+    each_late(lambda kind, shift: first_arrival(kind, shift).wait_recv())
+    ghost = ghost + first_flow(0, len(LATE))
+    total[...] = ghost
     solve_in[...] = known - ghost
+    each_peer(lambda kind, shift: first_arrival(kind, shift).wait_send())
     pulls[8].wait()
 
     chunk = 27
@@ -335,10 +359,9 @@
         lax.fori_loop(0, BLOCK // chunk, rows, 0)
 
     lanes8 = lax.broadcasted_iota(jnp.int32, (8, EL), 1)
+    tile_at = lanes8 // 8
     second = (lanes8 // 4) % 2
-    far_place = (lanes8 // 32) * 2 + second
-    tail = lax.broadcasted_iota(jnp.int32, (8, EL), 0) < BLOCK - 128
-
+    place_of = jnp.where(tile_at < 12, 2 * (tile_at // 6) + second, jnp.where(tile_at < 15, 4, 7))
     def merged(pieces, place):
         got = pieces[0]
         for part in range(1, len(pieces)):
@@ -349,38 +372,37 @@
         return jnp.concatenate([values, jnp.zeros((136 - BLOCK, EL), F32)], axis=0)
 
     def choose(level):
-        far_from = jnp.broadcast_to(far_lane[pl.ds(level, 1), :], (8, EL))
-
-        def row_of(i, target, where_from, place, parts):
-            for m in range(16 // parts):
-                pieces = [
-                    jnp.take_along_axis(
-                        inverse[i, 8 * (m * parts + part) : 8 * (m * parts + part + 1), :],
-                        where_from,
-                        axis=1,
+        where_from = jnp.broadcast_to(late_lane[pl.ds(level, 1), :], (8, EL))
+
+        def moved(values):
+            return jnp.take_along_axis(values, where_from, axis=1)
+
+        def rows(at, carry):
+            for k in range(chunk):
+                i = at * chunk + k
+                for m in range(3):
+                    late_chosen[i, 8 * m : 8 * m + 8, :] = merged(
+                        [
+                            moved(inverse[i, 8 * b : 8 * b + 8, :])
+                            for b in range(5 * m, 5 * m + 5)
+                        ],
+                        place_of,
                     )
-                    for part in range(parts)
-                ]
-                target[i, 8 * m : 8 * m + 8, :] = merged(pieces, place)
-            last = jnp.take_along_axis(tail_of(inverse[i, 128:BLOCK, :]), where_from, axis=1)
-            at = 128 // parts
-            target[i, at : at + 8, :] = jnp.where(tail, last, 0.0)
-
-        def far_rows(at, carry):
-            for k in range(chunk):
-                row_of(at * chunk + k, far_chosen, far_from, far_place, 8)
+                late_chosen[i, 24:32, :] = merged(
+                    [moved(inverse[i, 120:128, :]), moved(tail_of(inverse[i, 128:BLOCK, :]))],
+                    place_of,
+                )
             return carry
 
-        lax.fori_loop(0, BLOCK // chunk, far_rows, 0)
-
-    def fold(values, place, parts):
-        pieces = []
-        for m in range(16 // parts):
-            at = 8 * parts * m
-            pieces.append(
-                merged([values[at + 8 * p : at + 8 * p + 8] for p in range(parts)], place)
-            )
-        pieces.append(jnp.where(place == 0, tail_of(values[128:BLOCK]), 0.0))
+        lax.fori_loop(0, BLOCK // chunk, rows, 0)
+
+    def fold(values):
+        pieces = [
+            merged([values[8 * b : 8 * b + 8] for b in range(5 * m, 5 * m + 5)], place_of)
+            for m in range(3)
+        ]
+        last = merged([values[120:128], tail_of(values[128:BLOCK])], place_of)
+        pieces.append(jnp.where(place_of < 2, last, 0.0))
         return jnp.concatenate(pieces, axis=0)
 
     def part_multiply(chosen, vector, target):
@@ -404,12 +426,14 @@
 
         @pl.when(step >= 2)
         def _():
-            each_peer(lambda s, z: arrival(slot, s, z).wait_send())
+            each_peer(lambda kind, shift: arrival(slot, kind, shift).wait_send())
 
         fill_table()
-        out_buf[slot] = packed(level).reshape(GROUPS, 8, EL)
-        each_peer(lambda s, z: copy(slot, s, z).start())
-        in_buf[slot, own_group] = out_buf[slot, own_group]
+        fresh = packed(level).reshape(GROUPS, 8, EL)
+        out_buf[slot] = fresh - first_out[level]
+        each_peer(lambda kind, shift: copy(slot, kind, shift).start())
+        first_out[level] = fresh
+        in_buf[slot, here] = out_buf[slot, here]
 
         @pl.when(step == LEVELS - 1)
         def _():
@@ -418,41 +442,30 @@
         @pl.when(step > 0)
         def _():
             before = level_of(step - 1)
-            flow = near_flow[...] + scattered(
-                jnp.where(far_place[:1] == 0, far_spread[...], 0.0), far_drops[before]
-            )
-            flows[before] = flow
-            others[...] = others[...] + flow
-
-        @pl.when(step < LEVELS)
-        def _():
-            block = first_in[level].reshape(ROWS, EL)
-            flows[level] = scattered(spread(block, factors[level], 1), drops[level])
-
-        rest = others[...] - flows[level]
-        others[...] = rest
-        solve_in[...] = right_ref[...] - local_flow() - rest
+            once = jnp.where(place_of[:1] == 0, late_spread[...], 0.0)
+            total[...] = total[...] + early_flow[...] + scattered(once, late_drops[before])
+
+        solve_in[...] = right_ref[...] - local_flow() - total[...]
         choose(level)
-        each_near(lambda s, z: arrival(slot, s, z).wait_recv())
-        block = in_buf[slot, slabs:].reshape(ROWS - FAR, EL)
-        flow = scattered(spread(block, factors[level, FAR:], 1), drops[level, FAR:])
-        near_flow[...] = flow
+        each_early(lambda kind, shift: arrival(slot, kind, shift).wait_recv())
+        block = in_buf[slot, len(LATE) :].reshape(HALF, EL)
+        flow = scattered(spread(block, factors[level, HALF:]), drops[level, HALF:])
+        early_flow[...] = flow
         solve_in[...] = solve_in[...] - flow
         multiply()
-        each_far(lambda s, z: arrival(slot, s, z).wait_recv())
-        block = in_buf[slot, :slabs].reshape(FAR, EL)
-        values = spread(block, factors[level, :FAR], 4)
-        far_spread[...] = values
-        part_multiply(far_chosen, fold(values, far_place, 8), far_part)
-        fresh = update[...] - scattered(far_part[...], far_drops[level])
+        each_late(lambda kind, shift: arrival(slot, kind, shift).wait_recv())
+        block = in_buf[slot, : len(LATE)].reshape(HALF, EL)
+        values = spread(block, factors[level, :HALF], tiled)
+        late_spread[...] = values
+        part_multiply(late_chosen, fold(values), late_part)
+        fresh = update[...] - scattered(late_part[...], late_drops[level])
         state[...] = jnp.where(level_ref[...] == level_of(step + 1), fresh, state[...])
         return carry
 
     lax.fori_loop(0, 2 * LEVELS - 1, level_step, 0)
     swept_ref[...] = state[...]
-    each_peer(lambda s, z: first_arrival(s, z).wait_send())
     for slot in range(2):
-        each_peer(lambda s, z: arrival(slot, s, z).wait_send())
+        each_peer(lambda kind, shift: arrival(slot, kind, shift).wait_send())
 
 
 def hand_on(first_ref, second_ref, first_out, second_out, sems):
@@ -509,10 +522,9 @@
             pltpu.VMEM((8, EL), jnp.int32),
             pltpu.VMEM((BLOCK, EL), F32),
             pltpu.VMEM((BLOCK, EL), F32),
-            pltpu.VMEM((BLOCK, 24, EL), F32),
+            pltpu.VMEM((BLOCK, 32, EL), F32),
             pltpu.VMEM((BLOCK, EL), F32),
             pltpu.VMEM((LEVELS, ROWS, width), F32),
-            pltpu.VMEM((LEVELS, BLOCK, EL), F32),
             pltpu.VMEM((BLOCK, EL), F32),
             pltpu.VMEM((ROWS, EL), jnp.int32),
             pltpu.VMEM((2, GROUPS, 8, EL), F32),

time: 109 us -> 105 us (0.963)
  Pallas kernels: 108 us -> 105 us
    pallas_call x1, Pallas kernels: 106 us -> 103 us  [body(): pl.pallas_call(kernel, out_shape=(out, out), in_specs=[hbm] * 9, out_spec...]
where the time goes in v4:
time: 105 us
  Pallas kernels  105 us (100%)
    pallas_call x1, Pallas kernels, body(): pl.pallas_call(kernel, out_shape=(out, out), in_specs=[hbm] * 9, out_spec...  103 us

profile of v4, /device:TPU:7, one launch (start us, length us, event | category | flops | bytes accessed | tf_op | source)
XLA Modules:
  0.0 105.2 jit_solution(4339997075843933467)
XLA Ops:
  0.6 103.0 %shard_map.104 = (f32[135,128]{1,0:T(8,128)}, f32[135,128]{1,0:T(8,128)}) custom-call(f32[135,128]{1,0:T(8,128)} %start_hbm.1, f32[135,128]{1,0:T(8,128)} %right_hbm.1, f32[135,135,128]{2,1,0:T(8,128)} %inverse_hbm.1, f32[6,45,135]{2,1,0:T(8,128)} %bitcast.2, f32[6,128]{1,0:T(8,128)} %weight_hbm.1, s32[1,128]{1,0:T(1,128)} %bitcast.3, s32[6,128]{1,0:T(8,128)} %link_hbm.1, ...), custom_call_target="tpu_custom_call" | custom-call | tf_op jit(solution)/shard_map/pallas_call | solution.py:498
  103.6 1.6 %shard_map.105 = (f32[135,128]{1,0:T(8,128)}, f32[135,128]{1,0:T(8,128)}) custom-call(f32[135,128]{1,0:T(8,128)} %get-tuple-element.4.first_ref, f32[135,128]{1,0:T(8,128)} %get-tuple-element.5.second_ref), custom_call_target="tpu_custom_call" | custom-call | tf_op jit(solution)/shard_map/pallas_call | solution.py:554

commit v5 on v4

--- a/solution.py
+++ b/solution.py
@@ -21,6 +21,7 @@
 EARLY = ((OWN, 1), (OWN, 3), (PAIR, 1), (PAIR, 3), (PAIR, 0), (OWN, 0))
 PLACES = {key: at for at, key in enumerate(LATE + EARLY)}
 HALF = 8 * len(LATE)
+STACK = 144
 MESH = pl.DeviceIdType.MESH
 F32 = jnp.float32
 BF16 = jnp.bfloat16
@@ -65,6 +66,7 @@
     solve_in,
     update,
     jac,
+    jac2,
     jac3,
     links,
     picks,
@@ -198,10 +200,8 @@
 
     def packed(level):
         hi, lo = split(jnp.concatenate([table[face] for face in range(6)], axis=1))
-        both = jnp.concatenate([hi, lo], axis=1)
-        twice = jnp.concatenate([both, both], axis=0)
-        pick = picks[level]
-        return dot_t(jnp.concatenate([pick, pick], axis=1), twice)
+        halves = dot_t(picks[level], jnp.concatenate([hi, lo], axis=0))
+        return halves + pltpu.roll(halves, PAD, 1)
 
     for level in range(LEVELS):
         first_out[level] = packed(level).reshape(GROUPS, 8, EL)
@@ -270,6 +270,10 @@
         jac[PAD * face : PAD * face + TRACE, :BLOCK] = jac_ref[face]
     width = 6 * PAD
     jac_hi, jac_lo = split(jac[...].T[:BLOCK])
+    jac2[:BLOCK] = jac_hi
+    jac2[BLOCK:STACK] = jnp.zeros((STACK - BLOCK, width), BF16)
+    jac2[STACK : STACK + BLOCK] = jac_lo
+    jac2[STACK + BLOCK :] = jnp.zeros((STACK - BLOCK, width), BF16)
     jac3[:, :width] = jac_hi
     jac3[:, width : 2 * width] = jac_lo
     jac3[:, 2 * width :] = jac_hi
@@ -327,7 +331,8 @@
 
     def spread(block, factor, tile=lambda rows: rows):
         hi, lo = split(tile(jnp.concatenate([block] * 3, axis=1) * factor))
-        return dot_t(jac3[...], jnp.concatenate([hi, hi, lo], axis=1))
+        both = dot_t(jac2[...], hi)
+        return both[:BLOCK] + both[STACK : STACK + BLOCK] + dot_t(jac2[:BLOCK], lo)
 
     def first_flow(low, high):
         count = LEVELS * (high - low) * 8
@@ -345,18 +350,7 @@
     each_peer(lambda kind, shift: first_arrival(kind, shift).wait_send())
     pulls[8].wait()
 
-    chunk = 27
-
-    def multiply():
-        vector = solve_in[...]
-
-        def rows(at, carry):
-            for k in range(chunk):
-                i = at * chunk + k
-                update[pl.ds(i, 1), :] = jnp.sum(inverse[i] * vector, axis=0, keepdims=True)
-            return carry
-
-        lax.fori_loop(0, BLOCK // chunk, rows, 0)
+    chunk = 45
 
     lanes8 = lax.broadcasted_iota(jnp.int32, (8, EL), 1)
     tile_at = lanes8 // 8
@@ -381,14 +375,14 @@
             for k in range(chunk):
                 i = at * chunk + k
                 for m in range(3):
-                    late_chosen[i, 8 * m : 8 * m + 8, :] = merged(
+                    late_chosen[level, i, 8 * m : 8 * m + 8, :] = merged(
                         [
                             moved(inverse[i, 8 * b : 8 * b + 8, :])
                             for b in range(5 * m, 5 * m + 5)
                         ],
                         place_of,
                     )
-                late_chosen[i, 24:32, :] = merged(
+                late_chosen[level, i, 24:32, :] = merged(
                     [moved(inverse[i, 120:128, :]), moved(tail_of(inverse[i, 128:BLOCK, :]))],
                     place_of,
                 )
@@ -405,14 +399,70 @@
         pieces.append(jnp.where(place_of < 2, last, 0.0))
         return jnp.concatenate(pieces, axis=0)
 
-    def part_multiply(chosen, vector, target):
+    at8 = lax.broadcasted_iota(jnp.int32, (8, EL), 0)
+
+    def gathered_sums(parts):
+        top = at8 < 4
+        fours = [
+            jnp.where(top, parts[k], parts[k + 4])
+            + pltpu.roll(jnp.where(top, parts[k + 4], parts[k]), 4, 0)
+            for k in range(4)
+        ]
+        top = at8 % 4 < 2
+        twos = [
+            jnp.where(
+                top,
+                fours[k] + pltpu.roll(fours[k], 6, 0),
+                fours[k + 2] + pltpu.roll(fours[k + 2], 2, 0),
+            )
+            for k in range(2)
+        ]
+        return jnp.where(
+            at8 % 2 < 1, twos[0] + pltpu.roll(twos[0], 7, 0), twos[1] + pltpu.roll(twos[1], 1, 0)
+        )
+
+    def products(matrix, i, tiles):
+        got = None
+        for m, tile in enumerate(tiles):
+            one = matrix[i, 8 * m : 8 * m + 8, :] * tile
+            got = one if got is None else got + one
+        return got
+
+    def part_multiply(matrix, vector, target):
+        tiles = [vector[8 * m : 8 * m + 8] for m in range(4)]
+
         def rows(at, carry):
-            for k in range(chunk):
-                i = at * chunk + k
-                target[pl.ds(i, 1), :] = jnp.sum(chosen[i] * vector, axis=0, keepdims=True)
+            for k in range(8):
+                g = at * 8 + k
+                target[pl.ds(pl.multiple_of(8 * g, 8), 8), :] = gathered_sums(
+                    [products(matrix, 8 * g + r, tiles) for r in range(8)]
+                )
             return carry
 
-        lax.fori_loop(0, BLOCK // chunk, rows, 0)
+        lax.fori_loop(0, 16 // 8, rows, 0)
+        last = [products(matrix, 128 + r, tiles) for r in range(BLOCK - 128)]
+        target[128:BLOCK, :] = gathered_sums(last + [jnp.zeros((8, EL), F32)])[: BLOCK - 128]
+
+    def multiply():
+        vector = solve_in[...]
+        tiles = [vector[8 * m : 8 * m + 8] for m in range(16)]
+        last_tile = tail_of(vector[128:BLOCK])
+
+        def sums(i):
+            last = tail_of(inverse[i, 128:BLOCK, :]) * last_tile
+            return products(inverse, i, tiles) + last
+
+        def rows(at, carry):
+            for k in range(4):
+                g = at * 4 + k
+                update[pl.ds(pl.multiple_of(8 * g, 8), 8), :] = gathered_sums(
+                    [sums(8 * g + r) for r in range(8)]
+                )
+            return carry
+
+        lax.fori_loop(0, 4, rows, 0)
+        last = [sums(128 + r) for r in range(BLOCK - 128)]
+        update[128:BLOCK, :] = gathered_sums(last + [jnp.zeros((8, EL), F32)])[: BLOCK - 128]
 
     def level_of(step):
         return jnp.where(step < LEVELS, step, 2 * LEVELS - 1 - step)
@@ -446,7 +496,10 @@
             total[...] = total[...] + early_flow[...] + scattered(once, late_drops[before])
 
         solve_in[...] = right_ref[...] - local_flow() - total[...]
-        choose(level)
+        @pl.when(step < LEVELS)
+        def _():
+            choose(level)
+
         each_early(lambda kind, shift: arrival(slot, kind, shift).wait_recv())
         block = in_buf[slot, len(LATE) :].reshape(HALF, EL)
         flow = scattered(spread(block, factors[level, HALF:]), drops[level, HALF:])
@@ -457,7 +510,7 @@
         block = in_buf[slot, : len(LATE)].reshape(HALF, EL)
         values = spread(block, factors[level, :HALF], tiled)
         late_spread[...] = values
-        part_multiply(late_chosen, fold(values), late_part)
+        part_multiply(late_chosen.at[level], fold(values), late_part)
         fresh = update[...] - scattered(late_part[...], late_drops[level])
         state[...] = jnp.where(level_ref[...] == level_of(step + 1), fresh, state[...])
         return carry
@@ -514,6 +567,7 @@
             pltpu.VMEM((BLOCK, EL), F32),
             pltpu.VMEM((BLOCK, EL), F32),
             pltpu.VMEM((width, 256), F32),
+            pltpu.VMEM((2 * STACK, width), BF16),
             pltpu.VMEM((BLOCK, 3 * width), BF16),
             pltpu.VMEM((6, 2 * EL, EL), BF16),
             pltpu.VMEM((LEVELS, ROWS, 6 * EL), BF16),
@@ -522,7 +576,7 @@
             pltpu.VMEM((8, EL), jnp.int32),
             pltpu.VMEM((BLOCK, EL), F32),
             pltpu.VMEM((BLOCK, EL), F32),
-            pltpu.VMEM((BLOCK, 32, EL), F32),
+            pltpu.VMEM((LEVELS, BLOCK, 32, EL), F32),
             pltpu.VMEM((BLOCK, EL), F32),
             pltpu.VMEM((LEVELS, ROWS, width), F32),
             pltpu.VMEM((BLOCK, EL), F32),

time: 105 us -> 99.6 us (0.949)
  Pallas kernels: 105 us -> 98.5 us
    pallas_call x1, Pallas kernels: 103 us -> 96.9 us  [body(): pl.pallas_call(kernel, out_shape=(out, out), in_specs=[hbm] * 9, out_spec...]
where the time goes in v5:
time: 99.6 us; the launch traced here: 99.2 us
  Pallas kernels  98.5 us (99%)
    pallas_call x1, Pallas kernels, body(): pl.pallas_call(kernel, out_shape=(out, out), in_specs=[hbm] * 9, out_spec...  96.9 us

profile of v5, /device:TPU:7, one launch (start us, length us, event | category | flops | bytes accessed | tf_op | source)
XLA Modules:
  0.0 99.2 jit_solution(5924326279329988324)
XLA Ops:
  0.6 96.9 %shard_map.104 = (f32[135,128]{1,0:T(8,128)}, f32[135,128]{1,0:T(8,128)}) custom-call(f32[135,128]{1,0:T(8,128)} %start_hbm.1, f32[135,128]{1,0:T(8,128)} %right_hbm.1, f32[135,135,128]{2,1,0:T(8,128)} %inverse_hbm.1, f32[6,45,135]{2,1,0:T(8,128)} %bitcast.2, f32[6,128]{1,0:T(8,128)} %weight_hbm.1, s32[1,128]{1,0:T(1,128)} %bitcast.3, s32[6,128]{1,0:T(8,128)} %link_hbm.1, ...), custom_call_target="tpu_custom_call" | custom-call | tf_op jit(solution)/shard_map/pallas_call | solution.py:551
  97.6 1.6 %shard_map.105 = (f32[135,128]{1,0:T(8,128)}, f32[135,128]{1,0:T(8,128)}) custom-call(f32[135,128]{1,0:T(8,128)} %get-tuple-element.4.first_ref, f32[135,128]{1,0:T(8,128)} %get-tuple-element.5.second_ref), custom_call_target="tpu_custom_call" | custom-call | tf_op jit(solution)/shard_map/pallas_call | solution.py:608

commit v6 on v5

--- a/solution.py
+++ b/solution.py
@@ -432,14 +432,14 @@
         tiles = [vector[8 * m : 8 * m + 8] for m in range(4)]
 
         def rows(at, carry):
-            for k in range(8):
-                g = at * 8 + k
+            for k in range(16):
+                g = at * 16 + k
                 target[pl.ds(pl.multiple_of(8 * g, 8), 8), :] = gathered_sums(
                     [products(matrix, 8 * g + r, tiles) for r in range(8)]
                 )
             return carry
 
-        lax.fori_loop(0, 16 // 8, rows, 0)
+        rows(0, 0)
         last = [products(matrix, 128 + r, tiles) for r in range(BLOCK - 128)]
         target[128:BLOCK, :] = gathered_sums(last + [jnp.zeros((8, EL), F32)])[: BLOCK - 128]
 
@@ -474,16 +474,16 @@
         level = level_of(step)
         slot = lax.rem(step, 2)
 
-        @pl.when(step >= 2)
-        def _():
-            each_peer(lambda kind, shift: arrival(slot, kind, shift).wait_send())
-
         fill_table()
         fresh = packed(level).reshape(GROUPS, 8, EL)
         out_buf[slot] = fresh - first_out[level]
         each_peer(lambda kind, shift: copy(slot, kind, shift).start())
         first_out[level] = fresh
         in_buf[slot, here] = out_buf[slot, here]
+
+        @pl.when(step >= 1)
+        def _():
+            each_peer(lambda kind, shift: arrival(1 - slot, kind, shift).wait_send())
 
         @pl.when(step == LEVELS - 1)
         def _():
@@ -517,8 +517,7 @@
 
     lax.fori_loop(0, 2 * LEVELS - 1, level_step, 0)
     swept_ref[...] = state[...]
-    for slot in range(2):
-        each_peer(lambda kind, shift: arrival(slot, kind, shift).wait_send())
+    each_peer(lambda kind, shift: arrival(0, kind, shift).wait_send())
 
 
 def hand_on(first_ref, second_ref, first_out, second_out, sems):

time: 99.6 us -> 98.8 us (level)
  no operation moved by 1% of the time
where the time goes in v6:
time: 98.8 us; the launch traced here: 98.4 us
  Pallas kernels  97.8 us (99%)
    pallas_call x1, Pallas kernels, body(): pl.pallas_call(kernel, out_shape=(out, out), in_specs=[hbm] * 9, out_spec...  96.2 us

profile of v6, /device:TPU:7, one launch (start us, length us, event | category | flops | bytes accessed | tf_op | source)
XLA Modules:
  0.0 98.4 jit_solution(16258977836310526273)
XLA Ops:
  0.6 96.2 %shard_map.104 = (f32[135,128]{1,0:T(8,128)}, f32[135,128]{1,0:T(8,128)}) custom-call(f32[135,128]{1,0:T(8,128)} %start_hbm.1, f32[135,128]{1,0:T(8,128)} %right_hbm.1, f32[135,135,128]{2,1,0:T(8,128)} %inverse_hbm.1, f32[6,45,135]{2,1,0:T(8,128)} %bitcast.2, f32[6,128]{1,0:T(8,128)} %weight_hbm.1, s32[1,128]{1,0:T(1,128)} %bitcast.3, s32[6,128]{1,0:T(8,128)} %link_hbm.1, ...), custom_call_target="tpu_custom_call" | custom-call | tf_op jit(solution)/shard_map/pallas_call | solution.py:550
  96.8 1.6 %shard_map.105 = (f32[135,128]{1,0:T(8,128)}, f32[135,128]{1,0:T(8,128)}) custom-call(f32[135,128]{1,0:T(8,128)} %get-tuple-element.4.first_ref, f32[135,128]{1,0:T(8,128)} %get-tuple-element.5.second_ref), custom_call_target="tpu_custom_call" | custom-call | tf_op jit(solution)/shard_map/pallas_call | solution.py:607

commit v7 on v6

--- a/solution.py
+++ b/solution.py
@@ -82,8 +82,11 @@
     index,
     out_buf,
     in_buf,
+    sent,
     first_out,
     first_in,
+    first_drops,
+    first_factors,
     input_sems,
     send_sem,
     recv_sem,
@@ -123,7 +126,7 @@
     @pl.when(jnp.logical_not(has_far))
     def _():
         in_buf[:, :4] = jnp.zeros((2, 4, 8, EL), F32)
-        first_in[:, :4] = jnp.zeros((LEVELS, 4, 8, EL), F32)
+        first_in[:, :4] = jnp.zeros((LEVELS // 2, 4, 8, EL), F32)
 
     def each_late(act):
         @pl.when(has_far)
@@ -203,8 +206,12 @@
         halves = dot_t(picks[level], jnp.concatenate([hi, lo], axis=0))
         return halves + pltpu.roll(halves, PAD, 1)
 
-    for level in range(LEVELS):
-        first_out[level] = packed(level).reshape(GROUPS, 8, EL)
+    first_half = lax.broadcasted_iota(jnp.int32, (ROWS, EL), 0) % 8 < CAP
+    for duo in range(LEVELS // 2):
+        even, after = packed(2 * duo), packed(2 * duo + 1)
+        sent[2 * duo] = even.reshape(GROUPS, 8, EL)
+        sent[2 * duo + 1] = after.reshape(GROUPS, 8, EL)
+        first_out[duo] = jnp.where(first_half, even, after).reshape(GROUPS, 8, EL)
 
     @pl.when(has_far)
     def _():
@@ -294,7 +301,7 @@
 
     to_rows(recv_ref)
     face_lane = lax.broadcasted_iota(jnp.int32, (ROWS, width), 1) // PAD
-    first_half = lax.broadcasted_iota(jnp.int32, (ROWS, EL), 0) % 8 < CAP
+    wide_half = lax.broadcasted_iota(jnp.int32, (ROWS, width), 0) % 8 < CAP
     for level in range(LEVELS):
         column = index[:, level : level + 1]
         hit = jnp.zeros((ROWS, EL), F32)
@@ -306,7 +313,12 @@
         drops[level] = jnp.where(first_half, hit, 0.0).astype(BF16)
         late_drops[level] = tiled(hit[:HALF]).astype(BF16)
         scale = jnp.sum(gain, axis=1, keepdims=True)
-        factors[level] = jnp.where(column // EL == face_lane, scale, 0.0)
+        factor = jnp.where(column // EL == face_lane, scale, 0.0)
+        factors[level] = factor
+        if level % 2 == 1:
+            first_drops[level // 2] = jnp.where(first_half, even_hit, hit).astype(BF16)
+            first_factors[level // 2] = jnp.where(wide_half, even_factor, factor)
+        even_hit, even_factor = hit, factor
     late_lane[...] = (tiled(index[:HALF, :]).T)[:8] % EL
 
     def local_flow():
@@ -335,10 +347,10 @@
         return both[:BLOCK] + both[STACK : STACK + BLOCK] + dot_t(jac2[:BLOCK], lo)
 
     def first_flow(low, high):
-        count = LEVELS * (high - low) * 8
+        count = LEVELS // 2 * (high - low) * 8
         block = first_in[:, low:high].reshape(count, EL)
-        values = spread(block, factors[:, 8 * low : 8 * high].reshape(count, width))
-        return scattered(values, drops[:, 8 * low : 8 * high].reshape(count, EL))
+        values = spread(block, first_factors[:, 8 * low : 8 * high].reshape(count, width))
+        return scattered(values, first_drops[:, 8 * low : 8 * high].reshape(count, EL))
 
     known = right_ref[...] - local_flow()
     each_early(lambda kind, shift: first_arrival(kind, shift).wait_recv())
@@ -476,9 +488,9 @@
 
         fill_table()
         fresh = packed(level).reshape(GROUPS, 8, EL)
-        out_buf[slot] = fresh - first_out[level]
+        out_buf[slot] = fresh - sent[level]
         each_peer(lambda kind, shift: copy(slot, kind, shift).start())
-        first_out[level] = fresh
+        sent[level] = fresh
         in_buf[slot, here] = out_buf[slot, here]
 
         @pl.when(step >= 1)
@@ -583,7 +595,10 @@
             pltpu.VMEM((2, GROUPS, 8, EL), F32),
             pltpu.VMEM((2, GROUPS, 8, EL), F32),
             pltpu.VMEM((LEVELS, GROUPS, 8, EL), F32),
-            pltpu.VMEM((LEVELS, GROUPS, 8, EL), F32),
+            pltpu.VMEM((LEVELS // 2, GROUPS, 8, EL), F32),
+            pltpu.VMEM((LEVELS // 2, GROUPS, 8, EL), F32),
+            pltpu.VMEM((LEVELS // 2, ROWS, EL), BF16),
+            pltpu.VMEM((LEVELS // 2, ROWS, width), F32),
             pltpu.SemaphoreType.DMA((9,)),
             pltpu.SemaphoreType.DMA((2, GROUPS)),
             pltpu.SemaphoreType.DMA((2, GROUPS)),

time: 98.8 us -> 97.4 us (0.986)
  Pallas kernels: 97.8 us -> 96.6 us
    pallas_call x1, Pallas kernels: 96.2 us -> 95 us  [body(): pl.pallas_call(kernel, out_shape=(out, out), in_specs=[hbm] * 9, out_spec...]
where the time goes in v7:
time: 97.4 us; the launch traced here: 97.2 us
  Pallas kernels  96.6 us (99%)
    pallas_call x1, Pallas kernels, body(): pl.pallas_call(kernel, out_shape=(out, out), in_specs=[hbm] * 9, out_spec...  95 us

profile of v7, /device:TPU:7, one launch (start us, length us, event | category | flops | bytes accessed | tf_op | source)
XLA Modules:
  0.0 97.2 jit_solution(8242654860535868119)
XLA Ops:
  0.6 95.0 %shard_map.104 = (f32[135,128]{1,0:T(8,128)}, f32[135,128]{1,0:T(8,128)}) custom-call(f32[135,128]{1,0:T(8,128)} %start_hbm.1, f32[135,128]{1,0:T(8,128)} %right_hbm.1, f32[135,135,128]{2,1,0:T(8,128)} %inverse_hbm.1, f32[6,45,135]{2,1,0:T(8,128)} %bitcast.2, f32[6,128]{1,0:T(8,128)} %weight_hbm.1, s32[1,128]{1,0:T(1,128)} %bitcast.3, s32[6,128]{1,0:T(8,128)} %link_hbm.1, ...), custom_call_target="tpu_custom_call" | custom-call | tf_op jit(solution)/shard_map/pallas_call | solution.py:562
  95.6 1.6 %shard_map.105 = (f32[135,128]{1,0:T(8,128)}, f32[135,128]{1,0:T(8,128)}) custom-call(f32[135,128]{1,0:T(8,128)} %get-tuple-element.4.first_ref, f32[135,128]{1,0:T(8,128)} %get-tuple-element.5.second_ref), custom_call_target="tpu_custom_call" | custom-call | tf_op jit(solution)/shard_map/pallas_call | solution.py:622

commit v8 on v7

--- a/solution.py
+++ b/solution.py
@@ -353,16 +353,8 @@
         return scattered(values, first_drops[:, 8 * low : 8 * high].reshape(count, EL))
 
     known = right_ref[...] - local_flow()
-    each_early(lambda kind, shift: first_arrival(kind, shift).wait_recv())
-    ghost = first_flow(len(LATE), GROUPS)
-    each_late(lambda kind, shift: first_arrival(kind, shift).wait_recv())
-    ghost = ghost + first_flow(0, len(LATE))
-    total[...] = ghost
-    solve_in[...] = known - ghost
-    each_peer(lambda kind, shift: first_arrival(kind, shift).wait_send())
-    pulls[8].wait()
-
-    chunk = 45
+
+    chunk = 135
 
     lanes8 = lax.broadcasted_iota(jnp.int32, (8, EL), 1)
     tile_at = lanes8 // 8
@@ -465,20 +457,29 @@
             return products(inverse, i, tiles) + last
 
         def rows(at, carry):
-            for k in range(4):
-                g = at * 4 + k
+            for k in range(8):
+                g = at * 8 + k
                 update[pl.ds(pl.multiple_of(8 * g, 8), 8), :] = gathered_sums(
                     [sums(8 * g + r) for r in range(8)]
                 )
             return carry
 
-        lax.fori_loop(0, 4, rows, 0)
+        lax.fori_loop(0, 2, rows, 0)
         last = [sums(128 + r) for r in range(BLOCK - 128)]
         update[128:BLOCK, :] = gathered_sums(last + [jnp.zeros((8, EL), F32)])[: BLOCK - 128]
 
     def level_of(step):
         return jnp.where(step < LEVELS, step, 2 * LEVELS - 1 - step)
 
+    pulls[8].wait()
+    choose(0)
+    each_early(lambda kind, shift: first_arrival(kind, shift).wait_recv())
+    ghost = first_flow(len(LATE), GROUPS)
+    each_late(lambda kind, shift: first_arrival(kind, shift).wait_recv())
+    ghost = ghost + first_flow(0, len(LATE))
+    total[...] = ghost
+    solve_in[...] = known - ghost
+    each_peer(lambda kind, shift: first_arrival(kind, shift).wait_send())
     multiply()
     state[...] = jnp.where(level_ref[...] == 0, update[...], state[...])
 
@@ -508,9 +509,9 @@
             total[...] = total[...] + early_flow[...] + scattered(once, late_drops[before])
 
         solve_in[...] = right_ref[...] - local_flow() - total[...]
-        @pl.when(step < LEVELS)
+        @pl.when(step < LEVELS - 1)
         def _():
-            choose(level)
+            choose(level + 1)
 
         each_early(lambda kind, shift: arrival(slot, kind, shift).wait_recv())
         block = in_buf[slot, len(LATE) :].reshape(HALF, EL)

time: 97.4 us -> 96.8 us (level)
  no operation moved by 1% of the time
where the time goes in v8:
time: 96.8 us; the launch traced here: 96.7 us
  Pallas kernels  96 us (99%)
    pallas_call x1, Pallas kernels, body(): pl.pallas_call(kernel, out_shape=(out, out), in_specs=[hbm] * 9, out_spec...  94.5 us

profile of v8, /device:TPU:7, one launch (start us, length us, event | category | flops | bytes accessed | tf_op | source)
XLA Modules:
  0.0 96.7 jit_solution(14407701365713190286)
XLA Ops:
  0.6 94.5 %shard_map.104 = (f32[135,128]{1,0:T(8,128)}, f32[135,128]{1,0:T(8,128)}) custom-call(f32[135,128]{1,0:T(8,128)} %start_hbm.1, f32[135,128]{1,0:T(8,128)} %right_hbm.1, f32[135,135,128]{2,1,0:T(8,128)} %inverse_hbm.1, f32[6,45,135]{2,1,0:T(8,128)} %bitcast.2, f32[6,128]{1,0:T(8,128)} %weight_hbm.1, s32[1,128]{1,0:T(1,128)} %bitcast.3, s32[6,128]{1,0:T(8,128)} %link_hbm.1, ...), custom_call_target="tpu_custom_call" | custom-call | tf_op jit(solution)/shard_map/pallas_call | solution.py:563
  95.1 1.6 %shard_map.105 = (f32[135,128]{1,0:T(8,128)}, f32[135,128]{1,0:T(8,128)}) custom-call(f32[135,128]{1,0:T(8,128)} %get-tuple-element.4.first_ref, f32[135,128]{1,0:T(8,128)} %get-tuple-element.5.second_ref), custom_call_target="tpu_custom_call" | custom-call | tf_op jit(solution)/shard_map/pallas_call | solution.py:623

commit v9 on v8

--- a/solution.py
+++ b/solution.py
@@ -90,8 +90,6 @@
     input_sems,
     send_sem,
     recv_sem,
-    first_send_sem,
-    first_recv_sem,
 ):
     curves = lax.axis_size("curve")
     slabs = lax.axis_size("slab")
@@ -227,8 +225,8 @@
         return pltpu.make_async_remote_copy(
             src_ref=first_out.at[:, source],
             dst_ref=first_in.at[:, target],
-            send_sem=first_send_sem.at[source],
-            recv_sem=first_recv_sem.at[target],
+            send_sem=send_sem.at[1, source],
+            recv_sem=recv_sem.at[1, target],
             device_id=device(kind, shift),
             device_id_type=MESH,
         )
@@ -238,8 +236,8 @@
         return pltpu.make_async_remote_copy(
             src_ref=first_out.at[:, place],
             dst_ref=first_in.at[:, place],
-            send_sem=first_send_sem.at[place],
-            recv_sem=first_recv_sem.at[place],
+            send_sem=send_sem.at[1, place],
+            recv_sem=recv_sem.at[1, place],
             device_id=device(kind, shift),
             device_id_type=MESH,
         )
@@ -603,8 +601,6 @@
             pltpu.SemaphoreType.DMA((9,)),
             pltpu.SemaphoreType.DMA((2, GROUPS)),
             pltpu.SemaphoreType.DMA((2, GROUPS)),
-            pltpu.SemaphoreType.DMA((GROUPS,)),
-            pltpu.SemaphoreType.DMA((GROUPS,)),
         ],
         compiler_params=pltpu.CompilerParams(
             collective_id=0, has_side_effects=True, vmem_limit_bytes=60 << 20

time: 96.8 us -> 96.6 us (level)
  no operation moved by 1% of the time
where the time goes in v9:
time: 96.6 us; the launch traced here: 96.5 us
  Pallas kernels  95.8 us (99%)
    pallas_call x1, Pallas kernels, body(): pl.pallas_call(kernel, out_shape=(out, out), in_specs=[hbm] * 9, out_spec...  94.2 us

profile of v9, /device:TPU:7, one launch (start us, length us, event | category | flops | bytes accessed | tf_op | source)
XLA Modules:
  0.0 96.5 jit_solution(8366191406454273638)
XLA Ops:
  0.6 94.2 %shard_map.104 = (f32[135,128]{1,0:T(8,128)}, f32[135,128]{1,0:T(8,128)}) custom-call(f32[135,128]{1,0:T(8,128)} %start_hbm.1, f32[135,128]{1,0:T(8,128)} %right_hbm.1, f32[135,135,128]{2,1,0:T(8,128)} %inverse_hbm.1, f32[6,45,135]{2,1,0:T(8,128)} %bitcast.2, f32[6,128]{1,0:T(8,128)} %weight_hbm.1, s32[1,128]{1,0:T(1,128)} %bitcast.3, s32[6,128]{1,0:T(8,128)} %link_hbm.1, ...), custom_call_target="tpu_custom_call" | custom-call | tf_op jit(solution)/shard_map/pallas_call | solution.py:561
  94.9 1.6 %shard_map.105 = (f32[135,128]{1,0:T(8,128)}, f32[135,128]{1,0:T(8,128)}) custom-call(f32[135,128]{1,0:T(8,128)} %get-tuple-element.4.first_ref, f32[135,128]{1,0:T(8,128)} %get-tuple-element.5.second_ref), custom_call_target="tpu_custom_call" | custom-call | tf_op jit(solution)/shard_map/pallas_call | solution.py:619
